TPU v7x, 256 devices: a whole 4x4x8 slice. The times are simulated.
256 devices in a mesh: sect: 2 (over core), grp: 16 (over y_hi, z), tp: 8 (over y_lo, x).
Axes of the slice: x: 4, y: 4 (y_hi: 2, y_lo: 2; y = y_hi * 2 + y_lo), z: 8, core: 2. Of those that a mesh axis runs over, the one named last changes fastest.
Arguments:
- queries: bfloat16 [512, 128, 576], P('grp', ('sect', 'tp')), may hold values from -400 to 400, as said below
- latent_cache: bfloat16 [512, 128, 576], P('grp'), may hold values from -6 to 6, as said below
- cache_len: int32 [512], P('grp'), may hold values from 1 to 128, 32768 in all
- value_up: bfloat16 [128, 512, 128], P(('sect', 'tp')), may hold values from -0.25 to 0.25
- out_proj: bfloat16 [16384, 7168], P(('sect', 'tp'), 'grp'), may hold values from -0.046875 to 0.046875
- residual: bfloat16 [512, 7168], P(None, 'grp'), may hold values from -3 to 3
- w_gate: bfloat16 [16, 7168, 2048], P('grp', None, ('sect', 'tp')), may hold values from -0.0625 to 0.0625
- w_up: bfloat16 [16, 7168, 2048], P('grp', None, ('sect', 'tp')), may hold values from -0.0625 to 0.0625
- w_down: bfloat16 [16, 2048, 7168], P('grp', ('sect', 'tp')), may hold values from -0.1875 to 0.1875
- route_ids: int32 [512, 8], replicated, may hold values from 0 to 15, all different within a row; in each aligned block of 512 rows (0 to 511, 512 to 1023, ...) at most 384 rows name the same one
- route_weights: float32 [512, 8], replicated, may hold values from 0.1 to 0.6
Outputs:
- layer_out: bfloat16 [512, 7168], P(('sect', 'tp'), 'grp')
Inputs may be any that keep to these rules, and one draw needn't show every extreme that they name: `queries`: every entry lies in this range. `latent_cache`: every entry lies in this range. `route_ids`: each row names 8 different experts; every expert is named by at most 384 rows, and one expert by exactly 384. `cache_len`: some row has exactly 128 filled positions.
All inputs are finite; a program needn't handle non-finite values. No bound on the sum of `cache_len` on one device may be relied on, other than what follows from the above.
Results may differ from a plain program's by a relative error of at most 0.018.
Values may be sent and summed in bfloat16 or wider, within the bound.
A program may use at most 128 MiB of HBM per device.

v0:
```python
import jax
import jax.numpy as jnp
from jax import lax
from jax.sharding import PartitionSpec as P

LAT = 512
VDIM = 128
TOP = 8


SOFTMAX_SCALE = 0.0721688
MASK_VALUE = -1e30


def slot_tables(route_ids, route_weights, expert_count, capacity):
    row_total = route_ids.shape[0]
    expert_ids = jnp.arange(expert_count, dtype=jnp.int32)
    matches = route_ids[None, :, :] == expert_ids[:, None, None]
    chosen = jnp.any(matches, axis=2)
    weight = jnp.sum(jnp.where(matches, route_weights[None, :, :], 0.0), axis=2)
    slot_rank = jnp.cumsum(chosen.astype(jnp.int32), axis=1) - 1
    slot_ids = jnp.arange(capacity, dtype=jnp.int32)
    placed = chosen[:, :, None] & (slot_rank[:, :, None] == slot_ids[None, None, :])
    row_ids = jnp.arange(row_total, dtype=jnp.int32)
    slot_rows = jnp.sum(jnp.where(placed, row_ids[None, :, None], 0), axis=1)
    slot_valid = jnp.any(placed, axis=1)
    slot_weight = jnp.sum(jnp.where(placed, weight[:, :, None], 0.0), axis=1)
    return (placed, slot_rows, slot_valid, slot_weight)


def pick_slots(source_rows, slot_rows, slot_valid):
    picked = jnp.take(source_rows, slot_rows, axis=0)
    return jnp.where(slot_valid[:, :, None], picked, jnp.zeros_like(picked))


def on_device(
    queries,
    latent_cache,
    cache_len,
    value_up,
    out_proj,
    residual,
    w_gate,
    w_up,
    w_down,
    route_ids,
    route_weights,
):
    local_rows = queries.shape[0]
    local_heads = queries.shape[1]
    scores = (
        jnp.einsum("rhk,rlk->rhl", queries, latent_cache, preferred_element_type=jnp.float32)
        * SOFTMAX_SCALE
    )
    positions = jnp.arange(latent_cache.shape[1], dtype=jnp.int32)
    in_range = positions[None, None, :] < cache_len[:, None, None]
    masked = jnp.where(in_range, scores, MASK_VALUE)
    row_max = jnp.max(masked, axis=2, keepdims=True)
    exp_scores = jnp.where(in_range, jnp.exp(masked - row_max), 0.0)
    probs = (exp_scores / jnp.sum(exp_scores, axis=2, keepdims=True)).astype(jnp.bfloat16)
    latent_out = jnp.einsum(
        "rhl,rlc->rhc", probs, latent_cache[:, :, :LAT], preferred_element_type=jnp.float32
    ).astype(jnp.bfloat16)
    heads_out = jnp.einsum("rhc,hcv->rhv", latent_out, value_up, preferred_element_type=jnp.float32)
    heads_out = heads_out.astype(jnp.bfloat16).reshape(local_rows, local_heads * VDIM)
    partial_attn = jnp.dot(
        lax.all_gather(heads_out, "grp", axis=0, tiled=True),
        out_proj,
        preferred_element_type=jnp.float32,
    )
    row_total = residual.shape[0]
    expert_count = lax.axis_size("grp")
    tensor_count = lax.axis_size(("sect", "tp"))
    tensor_index = lax.axis_index(("sect", "tp"))
    own_expert = lax.axis_index("grp")
    capacity = min(row_total, row_total * TOP * 3 // (2 * expert_count))
    placed, slot_rows, slot_valid, slot_weight = slot_tables(
        route_ids, route_weights, expert_count, capacity
    )
    share_rows = row_total // tensor_count
    attention = lax.psum(partial_attn, ("sect", "tp"))
    layer_input = (residual.astype(jnp.float32) + attention).astype(jnp.bfloat16)
    own_rows = lax.dynamic_slice_in_dim(layer_input, tensor_index * share_rows, share_rows, 0)
    outgoing = pick_slots(layer_input, slot_rows, slot_valid)
    received = lax.all_to_all(outgoing, "grp", split_axis=0, concat_axis=2, tiled=True)
    expert_in = received[0]
    own_weight = lax.dynamic_index_in_dim(slot_weight, own_expert, 0, keepdims=False)
    gate_value = jnp.dot(expert_in, w_gate[0], preferred_element_type=jnp.float32)
    up_value = jnp.dot(expert_in, w_up[0], preferred_element_type=jnp.float32)
    hidden = (own_weight[:, None] * jax.nn.silu(gate_value) * up_value).astype(jnp.bfloat16)
    own_placed = lax.dynamic_index_in_dim(placed, own_expert, 0, keepdims=False).astype(
        jnp.bfloat16
    )
    hidden_rows = jnp.dot(own_placed, hidden, preferred_element_type=jnp.float32).astype(
        jnp.bfloat16
    )
    expert_term = jnp.dot(hidden_rows, w_down[0], preferred_element_type=jnp.float32)
    column_sums = lax.psum_scatter(
        expert_term.astype(jnp.bfloat16), "grp", scatter_dimension=1, tiled=True
    )
    routed_sum = lax.psum_scatter(
        column_sums, ("sect", "tp"), scatter_dimension=0, tiled=True
    ).astype(jnp.float32)
    return (own_rows.astype(jnp.float32) + routed_sum).astype(jnp.bfloat16)


def solution(mesh):
    return jax.shard_map(
        on_device,
        mesh=mesh,
        in_specs=(
            P("grp", ("sect", "tp"), None),
            P("grp", None, None),
            P("grp"),
            P(("sect", "tp"), None, None),
            P(("sect", "tp"), "grp"),
            P(None, "grp"),
            P("grp", None, ("sect", "tp")),
            P("grp", None, ("sect", "tp")),
            P("grp", ("sect", "tp"), None),
            P(),
            P(),
        ),
        out_specs=P(("sect", "tp"), "grp"),
        check_vma=False,
    )
```

profile of v0, /device:TPU:24, one launch (start us, length us, event | category | flops | bytes accessed | tf_op | source)
XLA Modules:
  0.0 729.3 jit_solution(1491521176456997909)
XLA Ops:
  6.5 0.0 copy-start
  6.5 0.0 all-gather.2.cloned.1.call-start
  6.5 0.9 iota_compare_fusion.2
  7.4 0.0 copy-start.1
  7.4 0.0 copy-start.3
  7.4 3.5 fusion.33
  10.9 0.0 copy-start.2
  10.9 3.5 fusion.9
  14.3 0.0 copy-done.1
  14.3 0.4 fusion.22
  14.7 0.6 copy.63
  15.3 0.0 all-gather.2.cloned.1.call-update
  15.4 0.0 all-reduce.2.cloned.1.call-start
  15.4 0.0 copy-done.3
  15.4 0.1 fusion.28
  15.5 1.2 reduce-window.6
  16.7 0.2 slice_reduce_fusion
  16.9 0.1 copy_bitcast_fusion.1
  17.0 3.3 select_reduce_fusion
  20.4 75.0 %all-gather.2.cloned.1.call-done = bf16[512,1024]{1,0:T(8,128)(2,1)} async-done(((bf16[32,1024]{1,0:T(8,128)(2,1)}), bf16[512,1024]{1,0:T(8,128)(2,1)}) %all-gather.2.cloned.1.call-update) | async-done | bytes 1048592 | tf_op jit(solution)/shard_map/all_gather | solution.py:67
  95.4 3.2 fusion.34
  98.6 0.0 all-reduce.2.cloned.1.call-update
  98.6 0.0 copy-done.2
  98.6 0.2 copy.42
  98.8 5.1 fusion.1
  104.0 131.3 %all-reduce.2.cloned.1.call-done = f32[512,448]{1,0:T(8,128)} async-done(((f32[512,448]{1,0:T(8,128)}), f32[512,448]{1,0:T(8,128)}) %all-reduce.2.cloned.1.call-update) | async-done | bytes 917520 | tf_op jit(solution)/shard_map/psum | solution.py:81
  235.3 1.4 add_convert_fusion
  236.7 25.4 %gather_fusion = bf16[6144,448]{1,0:T(8,128)(2,1)} fusion(bf16[512,448]{1,0:T(8,128)(2,1)S(1)} %add_convert_fusion, s32[6144]{0:T(1024)S(1)} %broadcast_clamp_fusion), kind=kCustom, calls=%fused_computation | custom fusion | bytes 11034624 | tf_op jit(solution)/shard_map/jit(_take)/gather | solution.py:32
  262.1 8.3 %copy.49 = bf16[16,384,448]{1,2,0:T(8,128)(2,1)} copy(bf16[16,384,448]{2,1,0:T(8,128)(2,1)} %bitcast.52) | data formatting | bytes 11010048 | tf_op jit(solution)/shard_map/jit(_take)/gather | solution.py:32
  270.5 5.9 select_select_fusion
  276.3 0.0 copy-start.4
  276.3 10.1 %all-to-all-start = ((bf16[16,384,448]{1,2,0:T(8,128)(2,1)}), bf16[16,384,448]{1,2,0:T(8,128)(2,1)}, u32[]{:S(2)}, u32[]{:S(2)}) async-start(bf16[16,384,448]{1,2,0:T(8,128)(2,1)} %select_select_fusion), calls=%async_computation | async-start | bytes 11010048 | tf_op jit(solution)/shard_map/all_to_all | solution.py:85
  286.5 0.0 reduce-scatter.5.cloned.1.call-start
  286.5 0.0 copy-done.4
  286.5 0.1 select_reduce_fusion.2
  286.6 4.6 select_reduce_fusion.1
  291.2 113.3 %all-to-all-done = bf16[16,384,448]{1,2,0:T(8,128)(2,1)} async-done(((bf16[16,384,448]{1,2,0:T(8,128)(2,1)}), bf16[16,384,448]{1,2,0:T(8,128)(2,1)}, u32[]{:S(2)}, u32[]{:S(2)}) %all-to-all-start) | async-done | bytes 5505056 | tf_op jit(solution)/shard_map/all_to_all | solution.py:85
  404.6 0.0 copy-start.5
  404.6 4.9 fusion.7
  409.4 0.0 copy-done.5
  409.4 4.2 fusion.16
  413.7 0.0 copy-done
  413.7 5.4 convolution_convert_fusion
  419.1 0.0 reduce-scatter.5.cloned.1.call-update
  419.2 0.0 reduce-scatter.7.cloned.1.call-start
  419.2 230.0 %reduce-scatter.5.cloned.1.call-done = bf16[512,448]{0,1:T(8,128)(2,1)} async-done(((bf16[512,7168]{0,1:T(8,128)(2,1)}), bf16[512,448]{0,1:T(8,128)(2,1)}) %reduce-scatter.5.cloned.1.call-update) | async-done | bytes 458768 | tf_op jit(solution)/shard_map/reduce_scatter | solution.py:98
  649.3 2.0 copy.52
  651.3 0.0 reduce-scatter.7.cloned.1.call-update
  651.3 70.1 %reduce-scatter.7.cloned.1.call-done = bf16[32,448]{1,0:T(8,128)(2,1)} async-done(((bf16[512,448]{1,0:T(8,128)(2,1)}), bf16[32,448]{1,0:T(8,128)(2,1)}) %reduce-scatter.7.cloned.1.call-update) | async-done | bytes 28688 | tf_op jit(solution)/shard_map/reduce_scatter | solution.py:101
  721.4 1.4 add_convert_fusion.1
  (8 shorter events, 0.1 us)
Async XLA Ops:
  6.5 407.1 %copy-start = (bf16[1,128,7168]{2,1,0:T(8,128)(2,1)S(1)}, bf16[1,128,7168]{2,1,0:T(8,128)(2,1)}, u32[]{:S(2)}) copy-start(bf16[1,128,7168]{2,1,0:T(8,128)(2,1)} %param.19) | copy-start | bytes 5505028
  6.5 88.8 %all-gather.2.cloned.1.call-start = ((), (), s32[]{:S(2)}) async-start(), calls=%async_computation.3 | async-start | bytes 1114112 | tf_op jit(solution)/shard_map/all_gather | solution.py:67
  7.4 6.9 copy-start.1
  7.4 8.0 %copy-start.3 = (s32[512,8]{0,1:T(8,128)S(1)}, s32[512,8]{0,1:T(8,128)}, u32[]{:S(2)}) copy-start(s32[512,8]{0,1:T(8,128)} %param.20) | copy-start | bytes 49156
  10.9 87.7 %copy-start.2 = (bf16[512,448]{0,1:T(8,128)(2,1)S(1)}, bf16[512,448]{0,1:T(8,128)(2,1)}, u32[]{:S(2)}) copy-start(bf16[512,448]{0,1:T(8,128)(2,1)} %param.16) | copy-start | bytes 1376260
  15.4 220.0 %all-reduce.2.cloned.1.call-start = ((), (), s32[]{:S(2)}) async-start(), calls=%async_computation.4 | async-start | bytes 2097152 | tf_op jit(solution)/shard_map/psum | solution.py:81
  276.3 10.2 %copy-start.4 = (f32[512,8]{0,1:T(8,128)S(1)}, f32[512,8]{0,1:T(8,128)}, u32[]{:S(2)}) copy-start(f32[512,8]{0,1:T(8,128)} %param.21) | copy-start | bytes 49156
  276.3 128.2 %all-to-all-start = ((bf16[16,384,448]{1,2,0:T(8,128)(2,1)}), bf16[16,384,448]{1,2,0:T(8,128)(2,1)}, u32[]{:S(2)}, u32[]{:S(2)}) async-start(bf16[16,384,448]{1,2,0:T(8,128)(2,1)} %select_select_fusion), calls=%async_computation | async-start | bytes 11010048 | tf_op jit(solution)/shard_map/all_to_all | solution.py:85
  286.5 362.8 %reduce-scatter.5.cloned.1.call-start = ((), (), s32[]{:S(2)}) async-start(), calls=%async_computation.5 | async-start | bytes 7798784 | tf_op jit(solution)/shard_map/reduce_scatter | solution.py:98
  404.6 4.9 copy-start.5
  419.2 302.3 %reduce-scatter.7.cloned.1.call-start = ((), (), s32[]{:S(2)}) async-start(), calls=%async_computation.6 | async-start | bytes 557056 | tf_op jit(solution)/shard_map/reduce_scatter | solution.py:101
Sparse Core Ops, SparseCore 0:
  15.5 79.8 all-gather.1
  98.7 136.5 all-reduce.1
  419.3 229.9 reduce-scatter.4
  651.6 69.7 reduce-scatter.6
where the time goes:
time: 730 us; the launch traced here: 729 us
  waiting for transfers between devices  620 us (85%)
  local copies, waits for them, and re-layouts  36.9 us (5%)
  matrix products  25 us (3%)
  other arithmetic  24 us (3%)
  between operations  13.3 us (2%)
  starting transfers between devices  10.2 us (1%)
    reduce_scatter x1, waiting for transfers between devices, on_device(): lax.psum_scatter(expert_term.astype(jnp.bfloat16), 'grp', scatter_dimensi...  230 us
    psum x1, waiting for transfers between devices, on_device(): attention = lax.psum(partial_attn, ('sect', 'tp'))  131 us
    all_to_all x1, waiting for transfers between devices, on_device(): lax.all_to_all(outgoing, 'grp', split_axis=0, concat_axis=2, tiled=True)  113 us
    all_gather x1, waiting for transfers between devices, on_device(): lax.all_gather(heads_out, 'grp', axis=0, tiled=True)  75 us
    reduce_scatter x1, waiting for transfers between devices, on_device(): lax.psum_scatter(column_sums, ('sect', 'tp'), scatter_dimension=0, tiled=...  70.1 us
    gather x2, local copies, waits for them, and re-layouts, pick_slots(): picked = jnp.take(source_rows, slot_rows, axis=0)  33.8 us
  transfers between devices with their start and end apart: 5, of which 5 were waited for; matrix products, arithmetic and copies ran while one was open for 2% of the time, Pallas kernels for 0%

commit v1 on v0

v1 whole, which is shorter than its diff:
```python
import jax
import jax.numpy as jnp
from jax import lax
from jax.experimental import pallas as pl
from jax.experimental.pallas import tpu as pltpu
from jax.sharding import PartitionSpec as P

LAT = 512
VDIM = 128
NX = 4
NY = 4
NZ = 8
NT = 8
NG = 16
NST = 16
BR = 32
BC = 448

SOFTMAX_SCALE = 0.0721688
MASK_VALUE = -1e30
MESH = pl.DeviceIdType.MESH
BF16 = jnp.bfloat16
F32 = jnp.float32


def _here():
    s = lax.axis_index("sect")
    g = lax.axis_index("grp")
    t = lax.axis_index("tp")
    yh, z = g // NZ, g % NZ
    yl, x = t // NX, t % NX
    return s, g, t, yh, z, yl, x


def _remote(src, dst, send, recv, dev):
    return pltpu.make_async_remote_copy(
        src_ref=src, dst_ref=dst, send_sem=send, recv_sem=recv, device_id=dev, device_id_type=MESH
    )


def _signal_all(devs):
    barrier = pltpu.get_barrier_semaphore()
    for dev in devs:
        pl.semaphore_signal(barrier, inc=1, device_id=dev, device_id_type=MESH)
    pl.semaphore_wait(barrier, len(devs))


def _heads_kernel(own_ref, out_ref, send_sem, psend_sem, recv_sem, local_sem):
    s, g, t, yh, z, yl, x = _here()
    oh = 1 - yh
    right = {"grp": yh * NZ + (z + 1) % NZ}
    left = {"grp": yh * NZ + (z + NZ - 1) % NZ}
    across = {"grp": oh * NZ + z}
    _signal_all([right, left, across])

    def hop(src, slot, way):
        c = _remote(src, out_ref.at[slot], send_sem.at[slot, way], recv_sem.at[slot], (right, left)[way])
        c.start()
        sent.append(c)

    def landed(slot):
        _remote(own_ref, out_ref.at[slot], psend_sem, recv_sem.at[slot], right).wait_recv()

    sent = []
    keep = pltpu.make_async_copy(own_ref, out_ref.at[g], local_sem)
    keep.start()
    pc = _remote(own_ref, out_ref.at[g], psend_sem, recv_sem.at[g], across)
    pc.start()
    hop(own_ref, g, 0)
    hop(own_ref, g, 1)
    half = NZ // 2

    def near(k):
        slot = yh * NZ + (z + NZ - k) % NZ
        landed(slot)
        if k < half:
            hop(out_ref.at[slot], slot, 0)
        if k < half:
            slot = yh * NZ + (z + k) % NZ
            landed(slot)
            if k < half - 1:
                hop(out_ref.at[slot], slot, 1)

    def far(k):
        if k == 0:
            slot = oh * NZ + z
            landed(slot)
            hop(out_ref.at[slot], slot, 0)
            hop(out_ref.at[slot], slot, 1)
            return
        if k < half:
            slot = oh * NZ + (z + NZ - k) % NZ
            landed(slot)
            if k < half - 1:
                hop(out_ref.at[slot], slot, 0)
        slot = oh * NZ + (z + k) % NZ
        landed(slot)
        if k < half:
            hop(out_ref.at[slot], slot, 1)

    for k in range(half + 1):
        if k < half:
            near(k + 1)
        far(k)
    keep.wait()
    pc.wait_send()
    for c in sent:
        c.wait_send()


def gather_heads(heads):
    out = pl.pallas_call(
        _heads_kernel,
        out_shape=jax.ShapeDtypeStruct((NG,) + heads.shape, BF16),
        in_specs=[pl.BlockSpec(memory_space=pltpu.VMEM)],
        out_specs=pl.BlockSpec(memory_space=pltpu.VMEM),
        scratch_shapes=[
            pltpu.SemaphoreType.DMA((NG, 2)),
            pltpu.SemaphoreType.DMA,
            pltpu.SemaphoreType.DMA((NG,)),
            pltpu.SemaphoreType.DMA,
        ],
        compiler_params=pltpu.CompilerParams(collective_id=0, has_side_effects=True),
        name="gather_heads",
    )(heads)
    return out.reshape(NG * heads.shape[0], heads.shape[1])


def _spread_kernel(
    part_ref, res_ref, all_ref, own_ref, rbuf, bsend, brecv, ssend, srecv, ysend, yrecv, rsend, rrecv, psend, precv
):
    s, g, t, yh, z, yl, x = _here()
    y = yh * 2 + yl
    d = s * NT + t

    def st_dev(e):
        return {"sect": e // NT, "tp": e % NT}

    def y_dev(e):
        return {"grp": (e // 2) * NZ + z, "tp": (e % 2) * NX + x}

    def z_dev(e):
        return {"grp": yh * NZ + e}

    def x_dev(e):
        return {"tp": yl * NX + e}

    partner = {"sect": 1 - s}
    _signal_all(
        [st_dev((d + o) % NST) for o in range(1, NST)]
        + [z_dev((z + o) % NZ) for o in range(1, NZ)]
        + [y_dev((y + o) % NY) for o in range(1, NY)]
    )

    sent = []

    def start(c):
        c.start()
        sent.append(c)

    for o in range(1, NST):
        e = (d + o) % NST
        start(_remote(part_ref.at[e], rbuf.at[d], bsend.at[o], brecv.at[d], st_dev(e)))
    total = res_ref[...].astype(F32) + part_ref[d].astype(F32)
    for o in range(1, NST):
        e = (d + NST - o) % NST
        _remote(part_ref.at[e], rbuf.at[e], bsend.at[o], brecv.at[e], st_dev(e)).wait_recv()
        total = total + rbuf[e].astype(F32)
    mine = total.astype(BF16)
    own_ref[...] = mine
    all_ref[yh, z, s, t] = mine

    def wait_recv(ref, sem):
        _remote(ref, ref, psend.at[0], sem, partner).wait_recv()

    @pl.when(s == 0)
    def _():
        def piece(xx, yy):
            return all_ref.at[yy // 2, :, 0, (yy % 2) * NX + xx]

        mark = len(sent)
        block = all_ref.at[yh, z, 0, t]
        for o in range(1, NZ):
            start(_remote(block, block, ssend.at[o], srecv.at[z], z_dev((z + o) % NZ)))
        for o in range(1, NZ):
            e = (z + NZ - o) % NZ
            wait_recv(all_ref.at[yh, e, 0, t], srecv.at[e])

        def to_partner(p, i):
            start(_remote(p, p, psend.at[i], precv.at[i], partner))

        xr, xl = (x + 1) % NX, (x + NX - 1) % NX
        xo = (x + 2) % NX
        order = (0, 3, 1, 2)
        for o in order[1:]:
            p = piece(x, y)
            start(_remote(p, p, ysend.at[o], yrecv.at[o], y_dev((y + o) % NY)))
        for j, o in enumerate(order):
            p = piece(x, (y + NY - o) % NY)
            if o:
                wait_recv(p, yrecv.at[o])
            start(_remote(p, p, rsend.at[0, j], rrecv.at[0, j], x_dev(xr)))
            start(_remote(p, p, rsend.at[1, j], rrecv.at[1, j], x_dev(xl)))
            to_partner(p, j)
        for j, o in enumerate(order):
            yy = (y + NY - o) % NY
            p = piece(xl, yy)
            wait_recv(p, rrecv.at[0, j])
            if j % 2 == 0:
                start(_remote(p, p, rsend.at[2, j], rrecv.at[2, j], x_dev(xr)))
            to_partner(p, 4 + j)
            p = piece(xr, yy)
            wait_recv(p, rrecv.at[1, j])
            if j % 2 == 1:
                start(_remote(p, p, rsend.at[2, j], rrecv.at[2, j], x_dev(xl)))
            to_partner(p, 8 + j)
        for j, o in enumerate(order):
            p = piece(xo, (y + NY - o) % NY)
            wait_recv(p, rrecv.at[2, j])
            to_partner(p, 12 + j)
        for c in sent[mark:]:
            c.wait_send()
        del sent[mark:]

    @pl.when(s == 1)
    def _():
        def piece(zz, hh):
            return all_ref.at[hh, zz, 1]

        mark = len(sent)
        block = all_ref.at[yh, z, 1, t]
        for o in range(1, NX):
            start(_remote(block, block, ssend.at[o], srecv.at[o], x_dev((x + o) % NX)))
        for o in range(1, NX):
            e = (x + NX - o) % NX
            wait_recv(all_ref.at[yh, z, 1, yl * NX + e], srecv.at[o])

        def quad(yy):
            return all_ref.at[yy // 2, z, 1, pl.ds((yy % 2) * NX, NX)]

        for o in range(1, NY):
            p = quad(y)
            start(_remote(p, p, ysend.at[o], yrecv.at[o], y_dev((y + o) % NY)))
        for o in range(1, NY):
            wait_recv(quad((y + NY - o) % NY), yrecv.at[o])

        def to_partner(p, i):
            start(_remote(p, p, psend.at[i], precv.at[i], partner))

        zr, zl = (z + 1) % NZ, (z + NZ - 1) % NZ
        half = NZ // 2
        for h in range(2):
            p = piece(z, h)
            start(_remote(p, p, rsend.at[0, h], rrecv.at[0, h], z_dev(zr)))
            start(_remote(p, p, rsend.at[1, h], rrecv.at[1, h], z_dev(zl)))
            to_partner(p, h)
        for k in range(1, half):
            for h in range(2):
                p = piece((z + NZ - k) % NZ, h)
                wait_recv(p, rrecv.at[0, 2 * (k - 1) + h])
                if k < half - 1 or h == 0:
                    start(_remote(p, p, rsend.at[0, 2 * k + h], rrecv.at[0, 2 * k + h], z_dev(zr)))
                to_partner(p, 4 * k - 2 + h)
                p = piece((z + k) % NZ, h)
                wait_recv(p, rrecv.at[1, 2 * (k - 1) + h])
                if k < half - 1 or h == 1:
                    start(_remote(p, p, rsend.at[1, 2 * k + h], rrecv.at[1, 2 * k + h], z_dev(zl)))
                to_partner(p, 4 * k + h)
        for h in range(2):
            p = piece((z + half) % NZ, h)
            wait_recv(p, rrecv.at[h, 2 * (half - 1) + h])
            to_partner(p, 14 + h)
        for c in sent[mark:]:
            c.wait_send()
        del sent[mark:]

    for c in sent:
        c.wait_send()

    @pl.when(s == 0)
    def _():
        for i in range(2):
            wait_recv(all_ref.at[i, z, 1], precv.at[i])
        for k in range(1, NZ // 2):
            for h in range(2):
                wait_recv(all_ref.at[h, (z + NZ - k) % NZ, 1], precv.at[4 * k - 2 + h])
                wait_recv(all_ref.at[h, (z + k) % NZ, 1], precv.at[4 * k + h])
        for h in range(2):
            wait_recv(all_ref.at[h, (z + NZ // 2) % NZ, 1], precv.at[14 + h])

    @pl.when(s == 1)
    def _():
        for i, xx in enumerate((x, (x + NX - 1) % NX, (x + 1) % NX, (x + 2) % NX)):
            for j, o in enumerate((0, 3, 1, 2)):
                yy = (y + NY - o) % NY
                wait_recv(all_ref.at[yy // 2, :, 0, (yy % 2) * NX + xx], precv.at[4 * i + j])


def spread_rows(partial, residual):
    vmem = pl.BlockSpec(memory_space=pltpu.VMEM)
    dma = pltpu.SemaphoreType.DMA
    everything, own = pl.pallas_call(
        _spread_kernel,
        out_shape=(
            jax.ShapeDtypeStruct((2, NZ, 2, NT, BR, BC), BF16),
            jax.ShapeDtypeStruct((BR, BC), BF16),
        ),
        in_specs=[vmem, vmem],
        out_specs=(vmem, vmem),
        scratch_shapes=[
            pltpu.VMEM((NST, BR, BC), BF16),
            dma((NST,)),
            dma((NST,)),
            dma((NZ,)),
            dma((NZ,)),
            dma((NY,)),
            dma((NY,)),
            dma((3, NZ)),
            dma((3, NZ)),
            dma((16,)),
            dma((16,)),
        ],
        compiler_params=pltpu.CompilerParams(
            collective_id=1, has_side_effects=True, vmem_limit_bytes=32 * 1024 * 1024
        ),
        name="spread_rows",
    )(partial.reshape(NST, BR, BC), residual)
    return everything.reshape(NG, NST * BR, BC), own


def _expert_kernel(g_ref, x_ref, wg_ref, wu_ref, wd_ref, ids_ref, wts_ref, out_ref, acc_ref, hid_ref):
    i = pl.program_id(0)

    @pl.when(i == 0)
    def _():
        acc_ref[...] = jnp.zeros_like(acc_ref)

    @pl.when(i < NG)
    def _():
        w = jnp.concatenate([wg_ref[...], wu_ref[...]], axis=1)
        acc_ref[...] += jnp.dot(x_ref[0], w, preferred_element_type=F32)

    @pl.when(i == NG)
    def _():
        g = g_ref[0]
        weight = jnp.sum(jnp.where(ids_ref[...] == g, wts_ref[...], 0.0), axis=1, keepdims=True)
        gate = acc_ref[:, :128]
        up = acc_ref[:, 128:]
        hid_ref[...] = (weight * (gate / (1.0 + jnp.exp(-gate))) * up).astype(BF16)

    @pl.when((i >= NG) & (i % 2 == 0))
    def _():
        out_ref[0] = jnp.dot(hid_ref[...], wd_ref[:, :BC], preferred_element_type=F32).astype(BF16)

    @pl.when((i >= NG) & (i % 2 == 1))
    def _():
        out_ref[0] = jnp.dot(hid_ref[...], wd_ref[:, BC:], preferred_element_type=F32).astype(BF16)


def expert_terms(rows, w_gate, w_up, w_down, route_ids, route_weights):
    own = lax.axis_index("grp").astype(jnp.int32).reshape(1)
    n = rows.shape[1]
    grid_spec = pltpu.PrefetchScalarGridSpec(
        num_scalar_prefetch=1,
        grid=(2 * NG,),
        in_specs=[
            pl.BlockSpec((1, n, BC), lambda i, o: (jnp.minimum(i, NG - 1), 0, 0)),
            pl.BlockSpec((BC, 128), lambda i, o: (jnp.minimum(i, NG - 1), 0)),
            pl.BlockSpec((BC, 128), lambda i, o: (jnp.minimum(i, NG - 1), 0)),
            pl.BlockSpec((128, 2 * BC), lambda i, o: (0, jnp.maximum(i - NG, 0) // 2)),
            pl.BlockSpec((n, 8), lambda i, o: (0, 0)),
            pl.BlockSpec((n, 8), lambda i, o: (0, 0)),
        ],
        out_specs=pl.BlockSpec((1, n, BC), lambda i, o: (jnp.maximum(i - NG, 0), 0, 0)),
        scratch_shapes=[pltpu.VMEM((n, 256), F32), pltpu.VMEM((n, 128), BF16)],
    )
    return pl.pallas_call(
        _expert_kernel,
        out_shape=jax.ShapeDtypeStruct((NG, n, BC), BF16),
        grid_spec=grid_spec,
        compiler_params=pltpu.CompilerParams(vmem_limit_bytes=32 * 1024 * 1024),
        name="expert_terms",
    )(own, rows, w_gate, w_up, w_down, route_ids, route_weights)


def _combine_kernel(
    term_ref, own_ref, out_ref, pbuf, acc, ring, ybuf, fbuf, psend, precv, rsend, rrecv, ysend, yrecv, fsend, frecv
):
    s, g, t, yh, z, yl, x = _here()
    y = yh * 2 + yl

    def y_dev(e):
        return {"grp": (e // 2) * NZ + z, "tp": (e % 2) * NX + x}

    def z_dev(e):
        return {"grp": yh * NZ + e}

    def x_dev(e):
        return {"tp": yl * NX + e}

    partner = {"sect": 1 - s}
    _signal_all(
        [partner]
        + [x_dev((x + o) % NX) for o in range(1, NX)]
        + [y_dev((y + o) % NY) for o in range(1, NY)]
        + [z_dev((z + o) % NZ) for o in range(1, NZ)]
    )
    sent = []

    def start(c):
        c.start()
        sent.append(c)

    def wait_recv(ref, sem):
        _remote(ref, ref, psend.at[0], sem, partner).wait_recv()

    def add(dst, srcs, n=8):
        def step(i, carry):
            v = srcs[0][i].astype(F32)
            for r in srcs[1:]:
                v = v + r[i].astype(F32)
            dst[i] = v.astype(BF16)
            return carry

        lax.fori_loop(0, n, step, 0)

    def finish(pairs):
        v = own_ref[...].astype(F32)
        tot = None
        for r in pairs:
            w = r[...].astype(F32)
            tot = w if tot is None else tot + w
        out_ref[...] = (v + tot).astype(BF16)

    xs = ((x + 2) % NX, (x + 1) % NX, (x + NX - 1) % NX, x)
    zs = [(z + NZ // 2) % NZ]
    for k in range(NZ // 2 - 1, 0, -1):
        zs += [(z + k) % NZ, (z + NZ - k) % NZ]
    zs.append(z)
    ys = ((y + 2) % NY, (y + 1) % NY, (y + NY - 1) % NY, y)

    @pl.when(s == 0)
    def _():
        for i, zz in enumerate(zs):
            for h in range(2):
                start(
                    _remote(
                        term_ref.at[h, zz, 1], pbuf.at[h, zz], psend.at[2 * i + h], precv.at[2 * i + h], partner
                    )
                )

        def at(ref, i, j):
            yy = ys[j]
            return ref.at[yy // 2, :, (yy % 2) * NX + xs[i]]

        def own_part(i, j, more=()):
            yy = ys[j]
            wait_recv(at(pbuf, i, j), precv.at[4 * i + j])
            add(
                at(acc, i, j),
                [term_ref.at[yy // 2, :, 0, (yy % 2) * NX + xs[i]], at(pbuf, i, j)] + list(more),
            )

        mark = 0
        right, left = x_dev((x + 1) % NX), x_dev((x + NX - 1) % NX)
        for j in range(4):
            own_part(0, j)
            start(_remote(at(acc, 0, j), ring.at[j], rsend.at[j], rrecv.at[j], right if j % 2 == 0 else left))
        for j in range(4):
            for i, way, dev in ((1, 0, right), (2, 1, left)):
                if j % 2 == way:
                    wait_recv(ring.at[j], rrecv.at[j])
                    own_part(i, j, [ring.at[j]])
                else:
                    own_part(i, j)
                k = 4 + 4 * way + j
                start(_remote(at(acc, i, j), ring.at[k], rsend.at[k], rrecv.at[k], dev))
        for j in range(4):
            wait_recv(ring.at[4 + j], rrecv.at[4 + j])
            wait_recv(ring.at[8 + j], rrecv.at[8 + j])
            if j < 3:
                own_part(3, j, [ring.at[4 + j], ring.at[8 + j]])
                o = (2, 1, 3)[j]
                start(_remote(at(acc, 3, j), ybuf.at[o], ysend.at[o], yrecv.at[o], y_dev(ys[j])))
            else:
                for o in (2, 1, 3):
                    wait_recv(ybuf.at[o], yrecv.at[o])
                own_part(3, j, [ring.at[4 + j], ring.at[8 + j]] + [ybuf.at[o] for o in (2, 1, 3)])
        for o in range(1, NZ):
            e = (z + o) % NZ
            start(_remote(acc.at[yh, e, t], fbuf.at[o], fsend.at[o], frecv.at[o], z_dev(e)))
        for o in range(1, NZ):
            wait_recv(fbuf.at[o], frecv.at[o])
        finish([acc.at[yh, z, t]] + [fbuf.at[o] for o in range(1, NZ)])
        for c in sent[mark:]:
            c.wait_send()
        del sent[mark:]

    @pl.when(s == 1)
    def _():
        for i, xx in enumerate(xs):
            for j, yy in enumerate(ys):
                r = (yy // 2, slice(None), 0, (yy % 2) * NX + xx)
                start(
                    _remote(
                        term_ref.at[r],
                        pbuf.at[yy // 2, :, (yy % 2) * NX + xx],
                        psend.at[4 * i + j],
                        precv.at[4 * i + j],
                        partner,
                    )
                )

        def own_part(i, h, more=()):
            zz = zs[i]
            wait_recv(pbuf.at[h, zz], precv.at[2 * i + h])
            add(acc.at[h, zz], [term_ref.at[h, zz, 1], pbuf.at[h, zz]] + list(more))

        right, left = z_dev((z + 1) % NZ), z_dev((z + NZ - 1) % NZ)
        for h in range(2):
            own_part(0, h)
            start(_remote(acc.at[h, zs[0]], ring.at[h], rsend.at[h], rrecv.at[h], (right, left)[h]))
        for k in range(1, NZ // 2):
            for h in range(2):
                for way, dev in ((0, right), (1, left)):
                    i = 2 * k - 1 + way
                    prev = None
                    if k == 1:
                        if h == way:
                            prev = h
                    else:
                        prev = 2 + 4 * (k - 2) + 2 * way + h
                    if prev is None:
                        own_part(i, h)
                    else:
                        wait_recv(ring.at[prev], rrecv.at[prev])
                        own_part(i, h, [ring.at[prev]])
                    q = 2 + 4 * (k - 1) + 2 * way + h
                    start(_remote(acc.at[h, zs[i]], ring.at[q], rsend.at[q], rrecv.at[q], dev))
        for h in range(2):
            q = 2 + 4 * (NZ // 2 - 2) + h
            wait_recv(ring.at[q], rrecv.at[q])
            wait_recv(ring.at[q + 2], rrecv.at[q + 2])
            own_part(7, h, [ring.at[q], ring.at[q + 2]])

        def quad(yy):
            return acc.at[yy // 2, z, pl.ds((yy % 2) * NX, NX)]

        def qbuf(o):
            return ybuf.at[o, pl.ds(0, NX)]

        for o in (2, 1, 3):
            e = (y + o) % NY
            start(_remote(quad(e), qbuf(o), ysend.at[o], yrecv.at[o], y_dev(e)))
        for o in (2, 1, 3):
            wait_recv(qbuf(o), yrecv.at[o])
        add(quad(y), [quad(y)] + [qbuf(o) for o in (2, 1, 3)], NX)
        for o in range(1, NX):
            e = (x + o) % NX
            start(_remote(acc.at[yh, z, yl * NX + e], fbuf.at[o], fsend.at[o], frecv.at[o], x_dev(e)))
        for o in range(1, NX):
            wait_recv(fbuf.at[o], frecv.at[o])
        finish([acc.at[yh, z, t]] + [fbuf.at[o] for o in range(1, NX)])
        for c in sent:
            c.wait_send()


def combine_terms(terms, own):
    vmem = pl.BlockSpec(memory_space=pltpu.VMEM)
    dma = pltpu.SemaphoreType.DMA
    return pl.pallas_call(
        _combine_kernel,
        out_shape=jax.ShapeDtypeStruct((BR, BC), BF16),
        in_specs=[vmem, vmem],
        out_specs=vmem,
        scratch_shapes=[
            pltpu.VMEM((2, NZ, NT, BR, BC), BF16),
            pltpu.VMEM((2, NZ, NT, BR, BC), BF16),
            pltpu.VMEM((16, 8, BR, BC), BF16),
            pltpu.VMEM((4, 8, BR, BC), BF16),
            pltpu.VMEM((8, BR, BC), BF16),
            dma((16,)),
            dma((16,)),
            dma((16,)),
            dma((16,)),
            dma((4,)),
            dma((4,)),
            dma((8,)),
            dma((8,)),
        ],
        compiler_params=pltpu.CompilerParams(
            collective_id=2, has_side_effects=True, vmem_limit_bytes=48 * 1024 * 1024
        ),
        name="combine_terms",
    )(terms.reshape(2, NZ, 2, NT, BR, BC), own)


def on_device(
    queries,
    latent_cache,
    cache_len,
    value_up,
    out_proj,
    residual,
    w_gate,
    w_up,
    w_down,
    route_ids,
    route_weights,
):
    local_rows = queries.shape[0]
    local_heads = queries.shape[1]
    scores = (
        jnp.einsum("rhk,rlk->rhl", queries, latent_cache, preferred_element_type=F32) * SOFTMAX_SCALE
    )
    positions = jnp.arange(latent_cache.shape[1], dtype=jnp.int32)
    in_range = positions[None, None, :] < cache_len[:, None, None]
    masked = jnp.where(in_range, scores, MASK_VALUE)
    row_max = jnp.max(masked, axis=2, keepdims=True)
    exp_scores = jnp.where(in_range, jnp.exp(masked - row_max), 0.0)
    probs = (exp_scores / jnp.sum(exp_scores, axis=2, keepdims=True)).astype(BF16)
    latent_out = jnp.einsum(
        "rhl,rlc->rhc", probs, latent_cache[:, :, :LAT], preferred_element_type=F32
    ).astype(BF16)
    heads_out = jnp.einsum("rhc,hcv->rhv", latent_out, value_up, preferred_element_type=F32)
    heads_out = heads_out.astype(BF16).reshape(local_rows, local_heads * VDIM)
    partial_attn = jnp.dot(gather_heads(heads_out), out_proj, preferred_element_type=F32).astype(BF16)
    tensor_index = lax.axis_index(("sect", "tp"))
    own_residual = lax.dynamic_slice_in_dim(residual, tensor_index * BR, BR, 0)
    rows, own_rows = spread_rows(partial_attn, own_residual)
    terms = expert_terms(rows, w_gate[0], w_up[0], w_down[0], route_ids, route_weights)
    return combine_terms(terms, own_rows)


def solution(mesh):
    return jax.shard_map(
        on_device,
        mesh=mesh,
        in_specs=(
            P("grp", ("sect", "tp"), None),
            P("grp", None, None),
            P("grp"),
            P(("sect", "tp"), None, None),
            P(("sect", "tp"), "grp"),
            P(None, "grp"),
            P("grp", None, ("sect", "tp")),
            P("grp", None, ("sect", "tp")),
            P("grp", ("sect", "tp"), None),
            P(),
            P(),
        ),
        out_specs=P(("sect", "tp"), "grp"),
        check_vma=False,
    )
```

time: 730 us -> 162 us (0.22)
  the two profiles are of different devices: /device:TPU:24 before, /device:TPU:1 now
where the time goes in v1:
time: 162 us
  Pallas kernels  131 us (81%)
  local copies, waits for them, and re-layouts  20 us (12%)
  matrix products  10.1 us (6%)
    pallas_call x1, Pallas kernels, spread_rows(): pl.pallas_call(_spread_kernel, out_shape=(jax.ShapeDtypeStruct((2, NZ, 2,...  50.7 us
    pallas_call x1, Pallas kernels, combine_terms(): pl.pallas_call(_combine_kernel, out_shape=jax.ShapeDtypeStruct((BR, BC),...  41.9 us
    pallas_call x1, Pallas kernels, gather_heads(): pl.pallas_call(_heads_kernel, out_shape=jax.ShapeDtypeStruct((NG,) + head...  26.4 us
    unnamed x26, local copies, waits for them, and re-layouts  17.2 us
    pallas_call x1, Pallas kernels, expert_terms(): pl.pallas_call(_expert_kernel, out_shape=jax.ShapeDtypeStruct((NG, n, BC)...  11.7 us
    sub x1, matrix products, on_device(): exp_scores = jnp.where(in_range, jnp.exp(masked - row_max), 0.0)  3.41 us
    dot_general x1, matrix products, on_device(): jnp.einsum('rhl,rlc->rhc', probs, latent_cache[:, :, :LAT], preferred_ele...  3.4 us

profile of v1, /device:TPU:1, one launch (start us, length us, event | category | flops | bytes accessed | tf_op | source)
XLA Modules:
  0.0 161.8 jit_solution(4424484763800094409)
XLA Ops:
  0.0 0.0 copy-start
  0.0 0.8 iota_compare_fusion
  0.8 1.0 constant_dynamic-slice_fusion
  1.8 0.1 copy.18.res_ref
  1.9 0.0 copy-start.9
  1.9 0.0 copy-start.10
  1.9 3.4 %fusion.9 = (f32[32,8]{1,0:T(8,128)S(1)}, f32[32,8,128]{2,1,0:T(8,128)S(1)}) fusion(pred[32,128]{1,0:T(8,128)(4,1)S(1)} %iota_compare_fusion, bf16[32,8,576]{2,1,0:T(8,128)(2,1)} %param.11, bf16[32,128,576]{1,2,0:T(8,128)(2,1)} %param.12), kind=kOutput, calls=%fused_computation.17 | convolution fusion | flops 37912704 | bytes 5149696 | tf_op jit(solution)/shard_map/sub | solution.py:620
  5.3 3.4 %fusion.1 = bf16[32,8,512]{2,1,0:T(8,128)(2,1)S(1)} fusion(bf16[32,128,576]{1,2,0:T(8,128)(2,1)} %param.12, f32[32,8,128]{2,1,0:T(8,128)S(1)} %get-tuple-element.10, f32[32,8]{1,0:T(8,128)S(1)} %get-tuple-element.9), kind=kOutput, calls=%fused_computation.1 | convolution fusion | flops 33619968 | bytes 4588544 | tf_op jit(solution)/shard_map/rhl,rlc->rhc/dot_general | solution.py:622
  8.7 0.0 copy-done
  8.7 0.0 copy-start.4
  8.8 0.4 fusion.7
  9.1 0.6 copy.23
  9.7 0.0 copy-done.9
  9.7 0.9 copy.15.ids_ref
  10.6 0.0 copy-done.10
  10.6 0.8 copy.16.wts_ref
  11.4 26.4 %gather_heads.1 = bf16[16,32,1024]{2,1,0:T(8,128)(2,1)} custom-call(bf16[32,1024]{1,0:T(8,128)(2,1)} %bitcast.26), custom_call_target="tpu_custom_call" | custom-call | tf_op jit(solution)/shard_map/gather_heads/pallas_call | solution.py:112
  37.9 3.0 %convolution_convert_fusion = bf16[512,448]{0,1:T(8,128)(2,1)} fusion(bf16[512,1024]{1,0:T(8,128)(2,1)} %bitcast.25, bf16[1024,448]{0,1:T(8,128)(2,1)} %param.15), kind=kOutput, calls=%fused_computation.3 | convolution fusion | flops 469991424 | bytes 2424832 | tf_op jit(solution)/shard_map/dot_general | solution.py:627
  40.9 1.2 copy.13
  42.1 50.7 %spread_rows.1 = (bf16[2,8,2,8,32,448]{5,4,3,2,1,0:T(8,128)(2,1)S(1)}, bf16[32,448]{1,0:T(8,128)(2,1)S(1)}) custom-call(bf16[16,32,448]{2,1,0:T(8,128)(2,1)S(1)} %bitcast.21, bf16[32,448]{1,0:T(8,128)(2,1)S(1)} %copy.18.res_ref), custom_call_target="tpu_custom_call" | custom-call | tf_op jit(solution)/shard_map/spread_rows/pallas_call | solution.py:302
  92.8 0.0 copy-start.2
  92.8 3.2 %copy-done.2 = bf16[2,8,2,8,32,448]{5,4,3,2,1,0:T(8,128)(2,1)} copy-done((bf16[2,8,2,8,32,448]{5,4,3,2,1,0:T(8,128)(2,1)}, bf16[2,8,2,8,32,448]{5,4,3,2,1,0:T(8,128)(2,1)S(1)}, u32[]{:S(2)}) %copy-start.2) | copy-done | bytes 7340056
  96.0 0.0 copy-done.4
  96.0 0.0 copy-start.3
  96.0 3.4 %copy-done.3 = bf16[2,8,2,8,32,448]{5,4,3,2,1,0:T(8,128)(2,1)S(1)} copy-done((bf16[2,8,2,8,32,448]{5,4,3,2,1,0:T(8,128)(2,1)S(1)}, bf16[2,8,2,8,32,448]{5,4,3,2,1,0:T(8,128)(2,1)}, u32[]{:S(2)}) %copy-start.3) | copy-done | bytes 7340056
  99.4 0.0 copy-start.5
  99.4 1.5 copy-done.5
  100.9 0.0 copy-start.6
  100.9 1.5 copy-done.6
  102.4 0.0 copy-start.7
  102.4 0.9 copy-done.7
  103.3 0.0 copy-start.8
  103.3 0.9 copy-done.8
  104.3 11.7 %expert_terms.1 = bf16[16,512,448]{2,1,0:T(8,128)(2,1)S(1)} custom-call(s32[1]{0:T(128)} %bitcast.g_ref, bf16[16,512,448]{2,1,0:T(8,128)(2,1)S(1)} %bitcast.20, bf16[7168,128]{1,0:T(8,128)(2,1)S(1)} %bitcast.22, bf16[7168,128]{1,0:T(8,128)(2,1)S(1)} %bitcast.23, bf16[128,7168]{1,0:T(8,128)(2,1)S(1)} %bitcast.24, s32[512,8]{1,0:T(8,128)S(1)} %copy-done.7, ...), custom_call_target="tpu_custom_call" | custom-call | tf_op jit(solution)/shard_map/expert_terms/pallas_call | solution.py:377
  116.0 0.0 copy-start.1
  116.0 3.2 %copy-done.1 = bf16[16,512,448]{2,1,0:T(8,128)(2,1)} copy-done((bf16[16,512,448]{2,1,0:T(8,128)(2,1)}, bf16[16,512,448]{2,1,0:T(8,128)(2,1)S(1)}, u32[]{:S(2)}) %copy-start.1) | copy-done | bytes 7340056
  119.3 41.9 %combine_terms.1 = bf16[32,448]{1,0:T(8,128)(2,1)S(1)} custom-call(bf16[2,8,2,8,32,448]{5,4,3,2,1,0:T(8,128)(2,1)} %bitcast.19, bf16[32,448]{1,0:T(8,128)(2,1)S(1)} %get-tuple-element.8.own_ref), custom_call_target="tpu_custom_call" | custom-call | tf_op jit(solution)/shard_map/combine_terms/pallas_call | solution.py:571
  161.1 0.6 copy.25
Async XLA Ops:
  0.0 8.7 %copy-start = (bf16[8,512,128]{2,1,0:T(8,128)(2,1)S(1)}, bf16[8,512,128]{2,1,0:T(8,128)(2,1)}, u32[]{:S(2)}) copy-start(bf16[8,512,128]{2,1,0:T(8,128)(2,1)} %param.14) | copy-start | bytes 3145732
  1.9 7.8 %copy-start.9 = (s32[512,8]{0,1:T(8,128)S(1)}, s32[512,8]{0,1:T(8,128)}, u32[]{:S(2)}) copy-start(s32[512,8]{0,1:T(8,128)} %param.20) | copy-start | bytes 49156
  1.9 8.7 %copy-start.10 = (f32[512,8]{0,1:T(8,128)S(1)}, f32[512,8]{0,1:T(8,128)}, u32[]{:S(2)}) copy-start(f32[512,8]{0,1:T(8,128)} %param.21) | copy-start | bytes 49156
  8.7 87.3 %copy-start.4 = (bf16[1,7168,128]{2,1,0:T(8,128)(2,1)S(1)}, bf16[1,7168,128]{2,1,0:T(8,128)(2,1)}, u32[]{:S(2)}) copy-start(bf16[1,7168,128]{2,1,0:T(8,128)(2,1)} %param.17) | copy-start | bytes 5505028
  92.8 3.2 %copy-start.2 = (bf16[2,8,2,8,32,448]{5,4,3,2,1,0:T(8,128)(2,1)}, bf16[2,8,2,8,32,448]{5,4,3,2,1,0:T(8,128)(2,1)S(1)}, u32[]{:S(2)}) copy-start(bf16[2,8,2,8,32,448]{5,4,3,2,1,0:T(8,128)(2,1)S(1)} %get-tuple-element.7) | copy-start | bytes 22020100
  96.0 3.4 %copy-start.3 = (bf16[2,8,2,8,32,448]{5,4,3,2,1,0:T(8,128)(2,1)S(1)}, bf16[2,8,2,8,32,448]{5,4,3,2,1,0:T(8,128)(2,1)}, u32[]{:S(2)}) copy-start(bf16[2,8,2,8,32,448]{5,4,3,2,1,0:T(8,128)(2,1)} %copy-done.2) | copy-start | bytes 22020100
  99.4 1.5 copy-start.5
  100.9 1.5 copy-start.6
  102.4 0.9 copy-start.7
  103.3 0.9 copy-start.8
  116.0 3.2 %copy-start.1 = (bf16[16,512,448]{2,1,0:T(8,128)(2,1)}, bf16[16,512,448]{2,1,0:T(8,128)(2,1)S(1)}, u32[]{:S(2)}) copy-start(bf16[16,512,448]{2,1,0:T(8,128)(2,1)S(1)} %expert_terms.1) | copy-start | bytes 22020100

commit v2 on v0

v2 whole, which is shorter than its diff:
```python
import jax
import jax.numpy as jnp
from jax import lax
from jax.experimental import pallas as pl
from jax.experimental.pallas import tpu as pltpu
from jax.sharding import PartitionSpec as P

LAT = 512
VDIM = 128
NX = 4
NY = 4
NZ = 8
NT = 8
NG = 16
NST = 16
BR = 32
BC = 448

SOFTMAX_SCALE = 0.0721688
MASK_VALUE = -1e30
MESH = pl.DeviceIdType.MESH
BF16 = jnp.bfloat16
F32 = jnp.float32


def _here():
    s = lax.axis_index("sect")
    g = lax.axis_index("grp")
    t = lax.axis_index("tp")
    yh, z = g // NZ, g % NZ
    yl, x = t // NX, t % NX
    return s, g, t, yh, z, yl, x


def _remote(src, dst, send, recv, dev):
    return pltpu.make_async_remote_copy(
        src_ref=src, dst_ref=dst, send_sem=send, recv_sem=recv, device_id=dev, device_id_type=MESH
    )


def _signal_all(devs):
    barrier = pltpu.get_barrier_semaphore()
    for dev in devs:
        pl.semaphore_signal(barrier, inc=1, device_id=dev, device_id_type=MESH)
    pl.semaphore_wait(barrier, len(devs))


NPIECE = 16


def _layer_kernel(
    own_ref,
    oproj_ref,
    res_ref,
    wg_ref,
    wu_ref,
    wd_ref,
    ids_ref,
    wts_ref,
    out_ref,
    gbuf,
    obuf,
    wbuf,
    wdraw,
    wdbuf,
    resbuf,
    wcol,
    part,
    rbuf,
    mine,
    rows,
    hacc,
    hid,
    tsend,
    pbuf,
    acc,
    ring,
    ybuf,
    fbuf,
    wsem,
    hsend,
    hrecv,
    asend,
    bsend,
    brecv,
    ssend,
    srecv,
    ysend,
    yrecv,
    rsend,
    rrecv,
    psend,
    precv,
    cpsend,
    cprecv,
    crsend,
    crrecv,
    cysend,
    cyrecv,
    cfsend,
    cfrecv,
):
    s, g, t, yh, z, yl, x = _here()
    y = yh * 2 + yl
    d = s * NT + t
    oh = 1 - yh

    def st_dev(e):
        return {"sect": e // NT, "tp": e % NT}

    def y_dev(e):
        return {"grp": (e // 2) * NZ + z, "tp": (e % 2) * NX + x}

    def z_dev(e):
        return {"grp": yh * NZ + e}

    def x_dev(e):
        return {"tp": yl * NX + e}

    partner = {"sect": 1 - s}
    zr, zl = (z + 1) % NZ, (z + NZ - 1) % NZ
    xr, xl = (x + 1) % NX, (x + NX - 1) % NX
    xo = (x + 2) % NX

    loads = [
        pltpu.make_async_copy(wg_ref, wbuf.at[:, pl.ds(0, 128)], wsem.at[0]),
        pltpu.make_async_copy(wu_ref, wbuf.at[:, pl.ds(128, 128)], wsem.at[1]),
        pltpu.make_async_copy(wd_ref, wdraw, wsem.at[2]),
    ]
    for c in loads:
        c.start()

    _signal_all(
        [st_dev((d + o) % NST) for o in range(1, NST)]
        + [z_dev((z + o) % NZ) for o in range(1, NZ)]
        + [y_dev((y + o) % NY) for o in range(1, NY)]
    )

    sent = []

    def start(c):
        c.start()
        sent.append(c)

    def landed(ref, sem):
        _remote(ref, ref, asend.at[0], sem, partner).wait_recv()


    def hop(src, slot, q, way):
        start(
            _remote(
                src, gbuf.at[slot, q], hsend.at[slot, way, q], hrecv.at[slot, q], (z_dev(zr), z_dev(zl))[way]
            )
        )

    for q in range(2):
        h = own_ref.at[q]
        start(_remote(h, gbuf.at[g, q], asend.at[q], hrecv.at[g, q], {"grp": oh * NZ + z}))
        hop(h, g, q, 0)
        hop(h, g, q, 1)

    for c in range(8):
        obuf[pl.ds(128 * c, 128), :] = oproj_ref[:, pl.ds(128 * c, 128)].T
    window = pl.multiple_of((d // 4) * 128, 128)
    resbuf[...] = res_ref[:, pl.ds(window, 128)].T
    pick = (ids_ref[...] == g).astype(F32) * wts_ref[...]
    wcol[...] = jnp.broadcast_to(jnp.sum(pick, axis=0, keepdims=True), (8, NST * BR)).T

    def project(slots, blocks):
        lhs = blocks[0] if len(blocks) == 1 else jnp.concatenate(blocks, axis=0)
        p = jnp.dot(lhs, obuf[...], preferred_element_type=F32).astype(BF16)
        for i, e in enumerate(slots):
            part[e] = p[i * BR : (i + 1) * BR]

            @pl.when(e != d)
            def _():
                _remote(part.at[e], rbuf.at[d], bsend.at[e], brecv.at[d], st_dev(e)).start()

    def block(slot):
        return gbuf[slot].reshape(BR, gbuf.shape[3])

    half = NZ // 2

    def arrive(side, k):
        plane = (yh, oh)[side] * NZ
        if k == 0:
            slot = plane + z
            for q in range(2):
                landed(gbuf.at[slot, q], hrecv.at[slot, q])
                hop(gbuf.at[slot, q], slot, q, 0)
                hop(gbuf.at[slot, q], slot, q, 1)
            return [slot]
        slots = []
        for q in range(2):
            for way in range(2):
                reach = half if way == side else half - 1
                if k > reach:
                    continue
                slot = plane + ((z + NZ - k) % NZ if way == 0 else (z + k) % NZ)
                landed(gbuf.at[slot, q], hrecv.at[slot, q])
                if k < reach:
                    hop(gbuf.at[slot, q], slot, q, way)
                if q == 0:
                    slots.append(slot)
        return slots

    project([g], [own_ref[...].reshape(BR, gbuf.shape[3])])
    for side, k in ((0, 1), (0, 2), (1, 0), (0, 3), (1, 1), (0, 4), (1, 2), (1, 3), (1, 4)):
        slots = arrive(side, k)
        project(slots, [block(e) for e in slots])

    for c in loads:
        c.wait()
    for i in range(8):
        v = wdraw[:, pl.ds(2 * BC * i, 2 * BC)]
        wdbuf[2 * i] = v[:, :BC]
        wdbuf[2 * i + 1] = v[:, BC:]

    base = pl.multiple_of((d % 4) * BR, BR)
    total = resbuf[pl.ds(base, BR), :].astype(F32) + part[d].astype(F32)
    for o in range(1, NST):
        e = (d + NST - o) % NST
        landed(rbuf.at[e], brecv.at[e])
        total = total + rbuf[e].astype(F32)
    mine[...] = total.astype(BF16)
    rows[yh, z, s, t] = total.astype(BF16)
    hacc[...] = jnp.zeros_like(hacc)

    def weights(hh, zz):
        return wbuf[pl.ds(pl.multiple_of((hh * NZ + zz) * BC, BC), BC), :]

    def use_plane(k):
        count = 2 if k in (0, half) else 4

        def step(i, carry):
            hh = i % 2
            zz = (z + (i // 2) * 2 * k + NZ - k) % NZ
            a = rows[hh, zz, 1].reshape(8 * BR, BC)
            p = jnp.dot(a, weights(hh, zz), preferred_element_type=F32)
            hacc[1] += p.reshape(8, BR, 256)
            return carry

        lax.fori_loop(0, count, step, 0)

    def use_group(xx):
        def step(i, carry):
            hh = i // NZ
            zz = i % NZ
            a = jnp.concatenate([rows[hh, zz, 0, xx], rows[hh, zz, 0, NX + xx]], axis=0)
            return carry + jnp.dot(a, weights(hh, zz), preferred_element_type=F32)

        p = lax.fori_loop(0, NG, step, jnp.zeros((2 * BR, 256), F32))
        hacc[0, xx] = p[:BR]
        hacc[0, NX + xx] = p[BR:]

    order = (0, 3, 1, 2)

    @pl.when(s == 0)
    def _():
        def piece(xx, yy):
            return rows.at[yy // 2, :, 0, (yy % 2) * NX + xx]

        mark = len(sent)
        b = rows.at[yh, z, 0, t]
        for o in range(1, NZ):
            start(_remote(b, b, ssend.at[o], srecv.at[z], z_dev((z + o) % NZ)))
        for o in range(1, NZ):
            e = (z + NZ - o) % NZ
            landed(rows.at[yh, e, 0, t], srecv.at[e])

        def to_partner(p, i):
            start(_remote(p, p, psend.at[i], precv.at[i], partner))

        def other(k):
            if k in (0, half):
                for h in range(2):
                    landed(rows.at[h, (z + k) % NZ, 1], precv.at[h if k == 0 else 14 + h])
            else:
                for h in range(2):
                    landed(rows.at[h, (z + NZ - k) % NZ, 1], precv.at[4 * k - 2 + h])
                    landed(rows.at[h, (z + k) % NZ, 1], precv.at[4 * k + h])
            use_plane(k)

        for o in order[1:]:
            p = piece(x, y)
            start(_remote(p, p, ysend.at[o], yrecv.at[o], y_dev((y + o) % NY)))
        for j, o in enumerate(order):
            p = piece(x, (y + NY - o) % NY)
            if o:
                landed(p, yrecv.at[o])
            start(_remote(p, p, rsend.at[0, j], rrecv.at[0, j], x_dev(xr)))
            start(_remote(p, p, rsend.at[1, j], rrecv.at[1, j], x_dev(xl)))
            to_partner(p, j)
        use_group(x)
        for j, o in enumerate(order):
            yy = (y + NY - o) % NY
            p = piece(xl, yy)
            landed(p, rrecv.at[0, j])
            if j % 2 == 0:
                start(_remote(p, p, rsend.at[2, j], rrecv.at[2, j], x_dev(xr)))
            to_partner(p, 4 + j)
            p = piece(xr, yy)
            landed(p, rrecv.at[1, j])
            if j % 2 == 1:
                start(_remote(p, p, rsend.at[2, j], rrecv.at[2, j], x_dev(xl)))
            to_partner(p, 8 + j)
            if j == 1:
                other(0)
        use_group(xl)
        use_group(xr)
        other(1)
        for j, o in enumerate(order):
            p = piece(xo, (y + NY - o) % NY)
            landed(p, rrecv.at[2, j])
            to_partner(p, 12 + j)
        use_group(xo)
        for k in range(2, half + 1):
            other(k)
        for c in sent[mark:]:
            c.wait_send()
        del sent[mark:]

    @pl.when(s == 1)
    def _():
        def piece(zz, hh):
            return rows.at[hh, zz, 1]

        mark = len(sent)
        b = rows.at[yh, z, 1, t]
        for o in range(1, NX):
            start(_remote(b, b, ssend.at[o], srecv.at[o], x_dev((x + o) % NX)))
        for o in range(1, NX):
            e = (x + NX - o) % NX
            landed(rows.at[yh, z, 1, yl * NX + e], srecv.at[o])

        def quad(yy):
            return rows.at[yy // 2, z, 1, pl.ds((yy % 2) * NX, NX)]

        for o in range(1, NY):
            p = quad(y)
            start(_remote(p, p, ysend.at[o], yrecv.at[o], y_dev((y + o) % NY)))
        for o in range(1, NY):
            landed(quad((y + NY - o) % NY), yrecv.at[o])

        def to_partner(p, i):
            start(_remote(p, p, psend.at[i], precv.at[i], partner))

        def other(i, xx):
            for j, o in enumerate(order):
                yy = (y + NY - o) % NY
                landed(rows.at[yy // 2, :, 0, (yy % 2) * NX + xx], precv.at[4 * i + j])
            use_group(xx)

        for h in range(2):
            p = piece(z, h)
            start(_remote(p, p, rsend.at[0, h], rrecv.at[0, h], z_dev(zr)))
            start(_remote(p, p, rsend.at[1, h], rrecv.at[1, h], z_dev(zl)))
            to_partner(p, h)
        use_plane(0)
        for k in range(1, half):
            for h in range(2):
                p = piece((z + NZ - k) % NZ, h)
                landed(p, rrecv.at[0, 2 * (k - 1) + h])
                if k < half - 1 or h == 0:
                    start(_remote(p, p, rsend.at[0, 2 * k + h], rrecv.at[0, 2 * k + h], z_dev(zr)))
                to_partner(p, 4 * k - 2 + h)
                p = piece((z + k) % NZ, h)
                landed(p, rrecv.at[1, 2 * (k - 1) + h])
                if k < half - 1 or h == 1:
                    start(_remote(p, p, rsend.at[1, 2 * k + h], rrecv.at[1, 2 * k + h], z_dev(zl)))
                to_partner(p, 4 * k + h)
            use_plane(k)
            if k == 1:
                other(0, x)
            if k == 3:
                other(1, xl)
                other(2, xr)
        for h in range(2):
            p = piece((z + half) % NZ, h)
            landed(p, rrecv.at[h, 2 * (half - 1) + h])
            to_partner(p, 14 + h)
        use_plane(half)
        other(3, xo)
        for c in sent[mark:]:
            c.wait_send()
        del sent[mark:]

    gate = hacc[:, :, :, :128].reshape(NST * BR, 128)
    up = hacc[:, :, :, 128:].reshape(NST * BR, 128)
    weight = wcol[:, 0:1]
    hid[...] = (weight * (gate / (1.0 + jnp.exp(-gate))) * up).astype(BF16).reshape(2, NT, BR, 128)

    def down_plane(dst, sec, zz, hh):
        a = hid[sec].reshape(NT * BR, 128)
        p = jnp.dot(a, wdbuf[hh * NZ + zz], preferred_element_type=F32)
        dst[hh, zz] = p.astype(BF16).reshape(NT, BR, BC)

    def down_group(dst, sec, xx):
        a = jnp.concatenate([hid[sec, xx], hid[sec, NX + xx]], axis=0)

        def step(i, carry):
            p = jnp.dot(a, wdbuf[i], preferred_element_type=F32).astype(BF16)
            dst[i // NZ, i % NZ, xx] = p[:BR]
            dst[i // NZ, i % NZ, NX + xx] = p[BR:]
            return carry

        lax.fori_loop(0, NG, step, 0)

    def add(dst, srcs, n=8):
        def step(i, carry):
            v = dst[i].astype(F32)
            for r in srcs:
                v = v + r[i].astype(F32)
            dst[i] = v.astype(BF16)
            return carry

        lax.fori_loop(0, n, step, 0)

    def finish(refs):
        tot = refs[0][...].astype(F32)
        for r in refs[1:]:
            tot = tot + r[...].astype(F32)
        out_ref[...] = (mine[...].astype(F32) + tot).astype(BF16)

    xs = (xo, xr, xl, x)
    zs = [(z + half) % NZ]
    for k in range(half - 1, 0, -1):
        zs += [(z + k) % NZ, (z + NZ - k) % NZ]
    zs.append(z)
    ys = ((y + 2) % NY, (y + 1) % NY, (y + NY - 1) % NY, y)

    @pl.when(s == 0)
    def _():
        mark = len(sent)

        def give(i):
            for h in range(2):
                down_plane(tsend, 1, zs[i], h)
                n = 2 * i + h
                start(_remote(tsend.at[h, zs[i]], pbuf.at[h, zs[i]], cpsend.at[n], cprecv.at[n], partner))

        def at(ref, i, j):
            yy = ys[j]
            return ref.at[yy // 2, :, (yy % 2) * NX + xs[i]]

        def take(i, j, more=()):
            landed(at(pbuf, i, j), cprecv.at[4 * i + j])
            add(at(acc, i, j), [at(pbuf, i, j)] + list(more))

        right, left = x_dev(xr), x_dev(xl)
        give(0)
        down_group(acc, 0, xs[0])
        give(1)
        for j in range(4):
            take(0, j)
            start(_remote(at(acc, 0, j), ring.at[j], crsend.at[j], crrecv.at[j], right if j % 2 == 0 else left))
        down_group(acc, 0, xs[1])
        give(2)
        down_group(acc, 0, xs[2])
        give(3)
        for j in range(4):
            for i, way, dev in ((1, 0, right), (2, 1, left)):
                if j % 2 == way:
                    landed(ring.at[j], crrecv.at[j])
                    take(i, j, [ring.at[j]])
                else:
                    take(i, j)
                k = 4 + 4 * way + j
                start(_remote(at(acc, i, j), ring.at[k], crsend.at[k], crrecv.at[k], dev))
            give(4 + j)
        down_group(acc, 0, xs[3])
        for j in range(4):
            landed(ring.at[4 + j], crrecv.at[4 + j])
            landed(ring.at[8 + j], crrecv.at[8 + j])
            take(3, j, [ring.at[4 + j], ring.at[8 + j]])
            if j < 3:
                o = (2, 1, 3)[j]
                start(_remote(at(acc, 3, j), ybuf.at[o], cysend.at[o], cyrecv.at[o], y_dev(ys[j])))
        for o in (2, 1, 3):
            landed(ybuf.at[o], cyrecv.at[o])
        add(at(acc, 3, 3), [ybuf.at[o] for o in (2, 1, 3)])
        for o in range(1, NZ):
            e = (z + o) % NZ
            start(_remote(acc.at[yh, e, t], fbuf.at[o], cfsend.at[o], cfrecv.at[o], z_dev(e)))
        for o in range(1, NZ):
            landed(fbuf.at[o], cfrecv.at[o])
        finish([acc.at[yh, z, t]] + [fbuf.at[o] for o in range(1, NZ)])
        for c in sent[mark:]:
            c.wait_send()
        del sent[mark:]

    @pl.when(s == 1)
    def _():
        mark = len(sent)

        def give(i):
            down_group(tsend, 0, xs[i])
            for j, yy in enumerate(ys):
                tt = (yy % 2) * NX + xs[i]
                n = 4 * i + j
                start(
                    _remote(tsend.at[yy // 2, :, tt], pbuf.at[yy // 2, :, tt], cpsend.at[n], cprecv.at[n], partner)
                )

        def have(i):
            for h in range(2):
                down_plane(acc, 1, zs[i], h)

        def take(i, h, more=()):
            landed(pbuf.at[h, zs[i]], cprecv.at[2 * i + h])
            add(acc.at[h, zs[i]], [pbuf.at[h, zs[i]]] + list(more))

        right, left = z_dev(zr), z_dev(zl)
        give(0)
        have(0)
        for h in range(2):
            take(0, h)
            start(_remote(acc.at[h, zs[0]], ring.at[h], crsend.at[h], crrecv.at[h], (right, left)[h]))
        give(1)
        have(1)
        have(2)
        give(2)
        for k in range(1, half):
            for h in range(2):
                for way, dev in ((0, right), (1, left)):
                    i = 2 * k - 1 + way
                    prev = None
                    if k == 1:
                        if h == way:
                            prev = h
                    else:
                        prev = 2 + 4 * (k - 2) + 2 * way + h
                    if prev is None:
                        take(i, h)
                    else:
                        landed(ring.at[prev], crrecv.at[prev])
                        take(i, h, [ring.at[prev]])
                    q = 2 + 4 * (k - 1) + 2 * way + h
                    start(_remote(acc.at[h, zs[i]], ring.at[q], crsend.at[q], crrecv.at[q], dev))
            if k == 1:
                give(3)
            have(2 * k + 1)
            if k < half - 1:
                have(2 * k + 2)
        for h in range(2):
            q = 2 + 4 * (half - 2) + h
            landed(ring.at[q], crrecv.at[q])
            landed(ring.at[q + 2], crrecv.at[q + 2])
            take(7, h, [ring.at[q], ring.at[q + 2]])

        def quad(yy):
            return acc.at[yy // 2, z, pl.ds((yy % 2) * NX, NX)]

        def qbuf(o):
            return ybuf.at[o, pl.ds(0, NX)]

        for o in (2, 1, 3):
            e = (y + o) % NY
            start(_remote(quad(e), qbuf(o), cysend.at[o], cyrecv.at[o], y_dev(e)))
        for o in (2, 1, 3):
            landed(qbuf(o), cyrecv.at[o])
        add(quad(y), [qbuf(o) for o in (2, 1, 3)], NX)
        for o in range(1, NX):
            e = (x + o) % NX
            start(_remote(acc.at[yh, z, yl * NX + e], fbuf.at[o], cfsend.at[o], cfrecv.at[o], x_dev(e)))
        for o in range(1, NX):
            landed(fbuf.at[o], cfrecv.at[o])
        finish([acc.at[yh, z, t]] + [fbuf.at[o] for o in range(1, NX)])
        for c in sent[mark:]:
            c.wait_send()
        del sent[mark:]

    for o in range(1, NST):
        e = (d + o) % NST
        _remote(part.at[e], rbuf.at[d], bsend.at[e], brecv.at[d], st_dev(e)).wait_send()
    for c in sent:
        c.wait_send()


def layer_rest(heads, out_proj, residual, w_gate, w_up, w_down, route_ids, route_weights):
    vmem = pl.BlockSpec(memory_space=pltpu.VMEM)
    hbm = pl.BlockSpec(memory_space=pl.ANY)
    dma = pltpu.SemaphoreType.DMA
    depth = heads.shape[1]
    scratch = [
        pltpu.VMEM((NG, 2, BR // 2, depth), BF16),
        pltpu.VMEM((depth, BC), BF16),
        pltpu.VMEM(w_gate.shape[:1] + (256,), BF16),
        pltpu.VMEM(w_down.shape, BF16),
        pltpu.VMEM((NG, 128, BC), BF16),
        pltpu.VMEM((128, BC), BF16),
        pltpu.VMEM((NST * BR, 8), F32),
        pltpu.VMEM((NST, BR, BC), BF16),
        pltpu.VMEM((NST, BR, BC), BF16),
        pltpu.VMEM((BR, BC), BF16),
        pltpu.VMEM((2, NZ, 2, NT, BR, BC), BF16),
        pltpu.VMEM((2, NT, BR, 256), F32),
        pltpu.VMEM((2, NT, BR, 128), BF16),
        pltpu.VMEM((2, NZ, NT, BR, BC), BF16),
        pltpu.VMEM((2, NZ, NT, BR, BC), BF16),
        pltpu.VMEM((2, NZ, NT, BR, BC), BF16),
        pltpu.VMEM((16, 8, BR, BC), BF16),
        pltpu.VMEM((4, 8, BR, BC), BF16),
        pltpu.VMEM((8, BR, BC), BF16),
        dma((3,)),
        dma((NG, 2, 2)),
        dma((NG, 2)),
        dma((2,)),
        dma((NST,)),
        dma((NST,)),
        dma((NZ,)),
        dma((NZ,)),
        dma((NY,)),
        dma((NY,)),
        dma((3, NZ)),
        dma((3, NZ)),
        dma((16,)),
        dma((16,)),
        dma((16,)),
        dma((16,)),
        dma((16,)),
        dma((16,)),
        dma((4,)),
        dma((4,)),
        dma((8,)),
        dma((8,)),
    ]
    return pl.pallas_call(
        _layer_kernel,
        out_shape=jax.ShapeDtypeStruct((BR, BC), BF16),
        in_specs=[vmem, vmem, vmem, hbm, hbm, hbm, vmem, vmem],
        out_specs=vmem,
        scratch_shapes=scratch,
        compiler_params=pltpu.CompilerParams(
            collective_id=0, has_side_effects=True, vmem_limit_bytes=60 * 1024 * 1024
        ),
        name="layer_rest",
    )(
        heads.reshape(2, BR // 2, depth),
        out_proj.T,
        residual.T,
        w_gate,
        w_up,
        w_down,
        route_ids.T,
        route_weights.T,
    )


def on_device(
    queries,
    latent_cache,
    cache_len,
    value_up,
    out_proj,
    residual,
    w_gate,
    w_up,
    w_down,
    route_ids,
    route_weights,
):
    local_rows = queries.shape[0]
    local_heads = queries.shape[1]
    scores = (
        jnp.einsum("rhk,rlk->rhl", queries, latent_cache, preferred_element_type=F32) * SOFTMAX_SCALE
    )
    positions = jnp.arange(latent_cache.shape[1], dtype=jnp.int32)
    in_range = positions[None, None, :] < cache_len[:, None, None]
    masked = jnp.where(in_range, scores, MASK_VALUE)
    row_max = jnp.max(masked, axis=2, keepdims=True)
    exp_scores = jnp.where(in_range, jnp.exp(masked - row_max), 0.0)
    probs = (exp_scores / jnp.sum(exp_scores, axis=2, keepdims=True)).astype(BF16)
    latent_out = jnp.einsum(
        "rhl,rlc->rhc", probs, latent_cache[:, :, :LAT], preferred_element_type=F32
    ).astype(BF16)
    heads_out = jnp.einsum("rhc,hcv->rhv", latent_out, value_up, preferred_element_type=F32)
    heads_out = heads_out.astype(BF16).reshape(local_rows, local_heads * VDIM)
    return layer_rest(
        heads_out, out_proj, residual, w_gate[0], w_up[0], w_down[0], route_ids, route_weights
    )


def solution(mesh):
    return jax.shard_map(
        on_device,
        mesh=mesh,
        in_specs=(
            P("grp", ("sect", "tp"), None),
            P("grp", None, None),
            P("grp"),
            P(("sect", "tp"), None, None),
            P(("sect", "tp"), "grp"),
            P(None, "grp"),
            P("grp", None, ("sect", "tp")),
            P("grp", None, ("sect", "tp")),
            P("grp", ("sect", "tp"), None),
            P(),
            P(),
        ),
        out_specs=P(("sect", "tp"), "grp"),
        check_vma=False,
    )
```

time: 730 us -> 127 us (0.17)
  the two profiles are of different devices: /device:TPU:24 before, /device:TPU:1 now
where the time goes in v2:
time: 127 us
  Pallas kernels  117 us (92%)
  matrix products  7.15 us (6%)
  local copies, waits for them, and re-layouts  2.06 us (2%)
    pallas_call x1, Pallas kernels, layer_rest(): pl.pallas_call(_layer_kernel, out_shape=jax.ShapeDtypeStruct((BR, BC), BF...  117 us
    dot_general x1, matrix products, on_device(): jnp.einsum('rhl,rlc->rhc', probs, latent_cache[:, :, :LAT], preferred_ele...  3.4 us
    sub x1, matrix products, on_device(): exp_scores = jnp.where(in_range, jnp.exp(masked - row_max), 0.0)  3.4 us

profile of v2, /device:TPU:1, one launch (start us, length us, event | category | flops | bytes accessed | tf_op | source)
XLA Modules:
  0.0 126.9 jit_solution(10857962587985446027)
XLA Ops:
  0.0 0.0 copy-start
  0.0 0.8 iota_compare_fusion
  0.8 3.4 %fusion.9 = (f32[32,8]{1,0:T(8,128)S(1)}, f32[32,8,128]{2,1,0:T(8,128)S(1)}) fusion(pred[32,128]{1,0:T(8,128)(4,1)S(1)} %iota_compare_fusion, bf16[32,8,576]{2,1,0:T(8,128)(2,1)} %param.11, bf16[32,128,576]{1,2,0:T(8,128)(2,1)} %param.12), kind=kOutput, calls=%fused_computation.14 | convolution fusion | flops 37912704 | bytes 5149696 | tf_op jit(solution)/shard_map/sub | solution.py:672
  4.2 3.4 %fusion.1 = bf16[32,8,512]{2,1,0:T(8,128)(2,1)S(1)} fusion(bf16[32,128,576]{1,2,0:T(8,128)(2,1)} %param.12, f32[32,8,128]{2,1,0:T(8,128)S(1)} %get-tuple-element.6, f32[32,8]{1,0:T(8,128)S(1)} %get-tuple-element.5), kind=kOutput, calls=%fused_computation.1 | convolution fusion | flops 33619968 | bytes 4588544 | tf_op jit(solution)/shard_map/rhl,rlc->rhc/dot_general | solution.py:674
  7.6 0.0 copy-done
  7.6 0.4 fusion.7
  8.0 0.7 reshape_reshape.3.own_ref
  8.7 116.8 %layer_rest.1 = bf16[32,448]{1,0:T(8,128)(2,1)} custom-call(bf16[2,16,1024]{2,1,0:T(8,128)(2,1)} %reshape_reshape.3.own_ref, bf16[448,1024]{1,0:T(8,128)(2,1)} %bitcast.15, bf16[448,512]{1,0:T(8,128)(2,1)} %bitcast.16, bf16[7168,128]{1,0:T(8,128)(2,1)} %bitcast.12, bf16[7168,128]{1,0:T(8,128)(2,1)} %bitcast.13, bf16[128,7168]{1,0:T(8,128)(2,1)} %bitcast.14, ...), custom_call_target="tpu_custom_call" | custom-call | tf_op jit(solution)/shard_map/layer_rest/pallas_call | solution.py:628
  125.5 1.4 %copy.17 = bf16[32,448]{1,0:T(8,128)(2,1)} copy(bf16[32,448]{1,0:T(8,128)(2,1)} %layer_rest.1) | data formatting | bytes 57344
  (1 shorter events, 0.0 us)
Async XLA Ops:
  0.0 7.6 %copy-start = (bf16[8,512,128]{2,1,0:T(8,128)(2,1)S(1)}, bf16[8,512,128]{2,1,0:T(8,128)(2,1)}, u32[]{:S(2)}) copy-start(bf16[8,512,128]{2,1,0:T(8,128)(2,1)} %param.14) | copy-start | bytes 3145732

commit v3 on v2

v3 whole, which is shorter than its diff:
```python
import jax
import jax.numpy as jnp
from jax import lax
from jax.experimental import pallas as pl
from jax.experimental.pallas import tpu as pltpu
from jax.sharding import PartitionSpec as P

LAT = 512
VDIM = 128
NX = 4
NY = 4
NZ = 8
NT = 8
NG = 16
NST = 16
BR = 32
BC = 448

SOFTMAX_SCALE = 0.0721688
MASK_VALUE = -1e30
MESH = pl.DeviceIdType.MESH
BF16 = jnp.bfloat16
F32 = jnp.float32


def _here():
    s = lax.axis_index("sect")
    g = lax.axis_index("grp")
    t = lax.axis_index("tp")
    yh, z = g // NZ, g % NZ
    yl, x = t // NX, t % NX
    return s, g, t, yh, z, yl, x


def _remote(src, dst, send, recv, dev):
    return pltpu.make_async_remote_copy(
        src_ref=src, dst_ref=dst, send_sem=send, recv_sem=recv, device_id=dev, device_id_type=MESH
    )


def _signal_all(devs):
    for dev in devs:
        pl.semaphore_signal(pltpu.get_barrier_semaphore(), inc=1, device_id=dev, device_id_type=MESH)
    return len(devs)


def _layer_kernel(
    len_ref,
    q_ref,
    cache_ref,
    vup_ref,
    oproj_ref,
    res_ref,
    wg_ref,
    wu_ref,
    wd_ref,
    ids_ref,
    wts_ref,
    out_ref,
    cbuf,
    vbuf,
    sbuf,
    lbuf,
    own_ref,
    gbuf,
    obuf,
    wbuf,
    wdraw,
    wdbuf,
    resbuf,
    wcol,
    part,
    rbuf,
    mine,
    rows,
    hacc,
    hid,
    tsend,
    pbuf,
    acc,
    ring,
    ybuf,
    fbuf,
    csem,
    wsem,
    hsend,
    hrecv,
    asend,
    bsend,
    brecv,
    ssend,
    srecv,
    ysend,
    yrecv,
    rsend,
    rrecv,
    psend,
    precv,
    cpsend,
    cprecv,
    crsend,
    crrecv,
    cysend,
    cyrecv,
    cfsend,
    cfrecv,
):
    s, g, t, yh, z, yl, x = _here()
    y = yh * 2 + yl
    d = s * NT + t
    oh = 1 - yh

    def st_dev(e):
        return {"sect": e // NT, "tp": e % NT}

    def y_dev(e):
        return {"grp": (e // 2) * NZ + z, "tp": (e % 2) * NX + x}

    def z_dev(e):
        return {"grp": yh * NZ + e}

    def x_dev(e):
        return {"tp": yl * NX + e}

    def xy_dev(ex, ey):
        return {"grp": (ey // 2) * NZ + z, "tp": (ey % 2) * NX + ex}

    partner = {"sect": 1 - s}
    zr, zl = (z + 1) % NZ, (z + NZ - 1) % NZ
    xr, xl = (x + 1) % NX, (x + NX - 1) % NX
    xo = (x + 2) % NX

    chunk = BR // 2
    fetch = [
        pltpu.make_async_copy(
            cache_ref.at[pl.ds(chunk * q, chunk)], cbuf.at[pl.ds(chunk * q, chunk)], csem.at[q]
        )
        for q in range(2)
    ]
    fetch.append(pltpu.make_async_copy(vup_ref, vbuf, csem.at[2]))
    for c in (fetch[0], fetch[2], fetch[1]):
        c.start()
    loads = [
        pltpu.make_async_copy(wg_ref, wbuf.at[:, pl.ds(0, 128)], wsem.at[0]),
        pltpu.make_async_copy(wu_ref, wbuf.at[:, pl.ds(128, 128)], wsem.at[1]),
        pltpu.make_async_copy(wd_ref, wdraw, wsem.at[2]),
    ]
    for c in loads:
        c.start()

    expected = _signal_all(
        [st_dev((d + o) % NST) for o in range(1, NST)]
        + [z_dev((z + o) % NZ) for o in range(1, NZ)]
        + [y_dev((y + o) % NY) for o in range(1, NY)]
        + [{"grp": oh * NZ + z, "tp": (t + o) % NT} for o in range(1, NT)]
    )

    sent = []

    def start(c):
        c.start()
        sent.append(c)

    def landed(ref, sem):
        _remote(ref, ref, asend.at[0], sem, partner).wait_recv()


    steps = [z_dev((z + o) % NZ) for o in (1, NZ - 1, 2, NZ - 2)] + [{"grp": oh * NZ + z}]

    def hop(src, slot, q, way):
        start(_remote(src, gbuf.at[slot, q], hsend.at[slot, q, way], hrecv.at[slot, q], steps[way]))

    def attend(q):
        fetch[q].wait()
        heads = q_ref.shape[1]
        shape = (heads, cbuf.shape[2])
        positions = lax.broadcasted_iota(jnp.int32, shape, 1)
        for i in range(chunk):
            r = chunk * q + i
            score = jnp.dot(q_ref[r], cbuf[r], preferred_element_type=F32) * SOFTMAX_SCALE
            sbuf[i] = jnp.where(positions < len_ref[r], score, MASK_VALUE)
        score = sbuf[...]
        top = jnp.max(score, axis=2, keepdims=True)
        e = jnp.where(score > 0.5 * MASK_VALUE, jnp.exp(score - top), 0.0)
        sbuf[...] = e / jnp.sum(e, axis=2, keepdims=True)
        for i in range(chunk):
            r = chunk * q + i
            latent = lax.dot_general(
                sbuf[i].astype(BF16), cbuf[r, :LAT], (((1,), (1,)), ((), ())), preferred_element_type=F32
            )
            lbuf[i] = latent.astype(BF16).astype(F32)
        if q == 0:
            fetch[2].wait()
        for h in range(heads):
            value = jnp.dot(lbuf[:, h, :].astype(BF16), vbuf[h], preferred_element_type=F32)
            own_ref[q, :, VDIM * h : VDIM * (h + 1)] = value.astype(BF16)

    for q in range(2):
        attend(q)
        if q == 0:
            pl.semaphore_wait(pltpu.get_barrier_semaphore(), expected)
        for way in (4, 2, 3, 0, 1):
            hop(own_ref.at[q], g, q, way)

    for c in range(8):
        obuf[pl.ds(128 * c, 128), :] = oproj_ref[:, pl.ds(128 * c, 128)].T
    window = pl.multiple_of((d // 4) * 128, 128)
    resbuf[...] = res_ref[:, pl.ds(window, 128)].T
    pick = (ids_ref[...] == g).astype(F32) * wts_ref[...]
    wcol[...] = jnp.broadcast_to(jnp.sum(pick, axis=0, keepdims=True), (8, NST * BR)).T

    def project(slots, blocks):
        lhs = blocks[0] if len(blocks) == 1 else jnp.concatenate(blocks, axis=0)
        p = jnp.dot(lhs, obuf[...], preferred_element_type=F32).astype(BF16)
        for i, e in enumerate(slots):
            part[e] = p[i * BR : (i + 1) * BR]

            @pl.when(e != d)
            def _():
                _remote(part.at[e], rbuf.at[d], bsend.at[e], brecv.at[d], st_dev(e)).start()

    def block(slot):
        return gbuf[slot].reshape(BR, gbuf.shape[3])

    half = NZ // 2

    def arrive(side, k):
        slots = []
        for q in range(2):
            for way in range(1 if k in (0, half) else 2):
                slot = (yh, oh)[side] * NZ + (z + NZ - k if way == 0 else z + k) % NZ
                landed(gbuf.at[slot, q], hrecv.at[slot, q])
                if side == 0 and k == 2:
                    hop(gbuf.at[slot, q], slot, q, way)
                    if q == way:
                        hop(gbuf.at[slot, q], slot, q, 2 + way)
                if side == 0 and k > 2:
                    hop(gbuf.at[slot, q], slot, q, 4)
                if side == 1 and k == 0:
                    for w in (2, 3, 0, 1):
                        hop(gbuf.at[slot, q], slot, q, w)
                if q == 0:
                    slots.append(slot)
        return slots

    held, blocks = [g], [own_ref[...].reshape(BR, gbuf.shape[3])]
    for side, k, now in (
        (0, 1, 0),
        (0, 2, 0),
        (1, 0, 1),
        (0, 3, 0),
        (0, 4, 1),
        (1, 1, 0),
        (1, 2, 1),
        (1, 3, 1),
        (1, 4, 1),
    ):
        slots = arrive(side, k)
        held += slots
        blocks += [block(e) for e in slots]
        if now:
            project(held, blocks)
            held, blocks = [], []

    for c in loads:
        c.wait()
    for i in range(8):
        v = wdraw[:, pl.ds(2 * BC * i, 2 * BC)]
        wdbuf[2 * i] = v[:, :BC]
        wdbuf[2 * i + 1] = v[:, BC:]

    base = pl.multiple_of((d % 4) * BR, BR)
    total = resbuf[pl.ds(base, BR), :].astype(F32) + part[d].astype(F32)
    for o in range(1, NST):
        e = (d + NST - o) % NST
        landed(rbuf.at[e], brecv.at[e])
        total = total + rbuf[e].astype(F32)
    mine[...] = total.astype(BF16)
    rows[yh, z, s, t] = total.astype(BF16)
    hacc[...] = jnp.zeros_like(hacc)

    def weights(hh, zz):
        return wbuf[pl.ds(pl.multiple_of((hh * NZ + zz) * BC, BC), BC), :]

    def use_plane(k):
        count = 2 if k in (0, half) else 4

        def step(i, carry):
            hh = i % 2
            zz = (z + (i // 2) * 2 * k + NZ - k) % NZ
            a = rows[hh, zz, 1].reshape(8 * BR, BC)
            p = jnp.dot(a, weights(hh, zz), preferred_element_type=F32)
            hacc[1] += p.reshape(8, BR, 256)
            return carry

        lax.fori_loop(0, count, step, 0)

    def use_group(*xx):
        places = [o + e for e in xx for o in (0, NX)]

        def step(i, carry):
            hh = i // NZ
            zz = i % NZ
            a = jnp.concatenate([rows[hh, zz, 0, e] for e in places], axis=0)
            return carry + jnp.dot(a, weights(hh, zz), preferred_element_type=F32)

        p = lax.fori_loop(0, NG, step, jnp.zeros((len(places) * BR, 256), F32))
        for i, e in enumerate(places):
            hacc[0, e] = p[i * BR : (i + 1) * BR]

    ymine = (y, (y + NY - 1) % NY, (y + 1) % NY, (y + 2) % NY)

    def quad_of(zz, yy):
        return rows.at[yy // 2, zz, 1, pl.ds((yy % 2) * NX, NX)]

    def qid(k, way, j):
        return j if k == 0 else 8 * k - 4 + 4 * way + j

    @pl.when(s == 0)
    def _():
        def piece(xx, yy):
            return rows.at[yy // 2, :, 0, (yy % 2) * NX + xx]

        mark = len(sent)
        b = rows.at[yh, z, 0, t]
        for o in range(1, NZ):
            start(_remote(b, b, ssend.at[o], srecv.at[z], z_dev((z + o) % NZ)))
        for o in range(1, NZ):
            e = (z + NZ - o) % NZ
            landed(rows.at[yh, e, 0, t], srecv.at[e])

        def to_partner(p, i):
            start(_remote(p, p, psend.at[i], precv.at[i], partner))

        def other(k):
            for j in range(4):
                for way in range(1 if k in (0, half) else 2):
                    landed(quad_of((z + NZ - k if way == 0 else z + k) % NZ, ymine[j]), precv.at[qid(k, way, j)])
            use_plane(k)

        yr, yl_ = y_dev((y + 1) % NY), y_dev((y + NY - 1) % NY)
        p = piece(x, y)
        start(_remote(p, p, ysend.at[0], yrecv.at[0], yr))
        start(_remote(p, p, ysend.at[1], yrecv.at[1], yl_))

        def out(j):
            q = piece(x, ymine[j])
            start(_remote(q, q, rsend.at[0, j], rrecv.at[0, j], x_dev(xr)))
            start(_remote(q, q, rsend.at[1, j], rrecv.at[1, j], x_dev(xl)))
            to_partner(q, j)

        def halfof(w):
            yy = ymine[(1, 2)[w]]
            return rows.at[yy // 2, pl.ds(4 * w, 4), 0, (yy % 2) * NX + x]

        def halfin(w):
            yy = ymine[3]
            return rows.at[yy // 2, pl.ds(4 * w, 4), 0, (yy % 2) * NX + x]

        def ring_in(j):
            q = piece(xl, ymine[j])
            landed(q, rrecv.at[0, j])
            if j % 2 == 0:
                start(_remote(q, q, rsend.at[0, 4 + j], rrecv.at[0, 4 + j], x_dev(xr)))
            to_partner(q, 4 + j)
            q = piece(xr, ymine[j])
            landed(q, rrecv.at[1, j])
            if j % 2 == 1:
                start(_remote(q, q, rsend.at[1, 4 + j], rrecv.at[1, 4 + j], x_dev(xl)))
            to_partner(q, 8 + j)

        out(0)
        for w in range(2):
            landed(piece(x, ymine[1 + w]), yrecv.at[w])
            q = halfof(w)
            start(_remote(q, q, ysend.at[2 + w], yrecv.at[2 + w], (yr, yl_)[w]))
            out(1 + w)
        ring_in(0)
        for w in range(2):
            landed(halfin(w), yrecv.at[2 + w])
        out(3)
        use_group(x)
        ring_in(1)
        ring_in(2)
        other(0)
        ring_in(3)
        use_group(xl, xr)
        other(1)
        for j in range(4):
            p = piece(xo, ymine[j])
            landed(p, rrecv.at[j % 2, 4 + j])
            to_partner(p, 12 + j)
        use_group(xo)
        for k in range(2, half + 1):
            other(k)
        for c in sent[mark:]:
            c.wait_send()
        del sent[mark:]

    @pl.when(s == 1)
    def _():
        def piece(zz, hh):
            return rows.at[hh, zz, 1]

        mark = len(sent)
        b = rows.at[yh, z, 1, t]
        for oy in (0, 1, 3, 2):
            for ox in range(NX):
                if oy + ox:
                    n = oy * NX + ox
                    start(_remote(b, b, ssend.at[n], srecv.at[n], xy_dev((x + ox) % NX, (y + oy) % NY)))

        def to_partner(p, i):
            start(_remote(p, p, psend.at[i], precv.at[i], partner))

        def other(i, *xx):
            for e in xx:
                for j in range(4):
                    yy = ymine[j]
                    landed(rows.at[yy // 2, :, 0, (yy % 2) * NX + e], precv.at[4 * i + j])
                i = i + 1
            use_group(*xx)

        def out(j):
            q = quad_of(z, ymine[j])
            start(_remote(q, q, rsend.at[0, j], rrecv.at[0, j], z_dev(zr)))
            start(_remote(q, q, rsend.at[1, j], rrecv.at[1, j], z_dev(zl)))
            to_partner(q, qid(0, 0, j))

        def ring_in(k, j):
            n = 4 * k + j
            for way in range(2):
                if k == half and j % 2 != way:
                    continue
                q = quad_of((z + NZ - k if way == 0 else z + k) % NZ, ymine[j])
                landed(q, rrecv.at[way, n - 4])
                if k < half - 1 or (k == half - 1 and j % 2 == way):
                    start(_remote(q, q, rsend.at[way, n], rrecv.at[way, n], z_dev((zr, zl)[way])))
                to_partner(q, qid(k, 0 if k == half else way, j))

        for j, oy in enumerate((0, 1, 3, 2)):
            yy = ymine[j]
            for ox in range(NX):
                if oy + ox:
                    n = oy * NX + ox
                    landed(rows.at[yy // 2, z, 1, (yy % 2) * NX + (x + NX - ox) % NX], srecv.at[n])
            out(j)
        use_plane(0)
        for k in range(1, half + 1):
            for j in range(4):
                ring_in(k, j)
            if k < half:
                use_plane(k)
            if k == 2:
                other(0, x)
            if k == 3:
                other(1, xl, xr)
        use_plane(half)
        other(3, xo)
        for c in sent[mark:]:
            c.wait_send()
        del sent[mark:]

    gate = hacc[:, :, :, :128].reshape(NST * BR, 128)
    up = hacc[:, :, :, 128:].reshape(NST * BR, 128)
    weight = wcol[:, 0:1]
    hid[...] = (weight * (gate / (1.0 + jnp.exp(-gate))) * up).astype(BF16).reshape(2, NT, BR, 128)

    def down_plane(dst, sec, zz, hh):
        a = hid[sec].reshape(NT * BR, 128)
        p = jnp.dot(a, wdbuf[hh * NZ + zz], preferred_element_type=F32)
        dst[hh, zz] = p.astype(BF16).reshape(NT, BR, BC)

    def down_group(dst, sec, xx):
        a = jnp.concatenate([hid[sec, xx], hid[sec, NX + xx]], axis=0)

        def step(i, carry):
            p = jnp.dot(a, wdbuf[i], preferred_element_type=F32).astype(BF16)
            dst[i // NZ, i % NZ, xx] = p[:BR]
            dst[i // NZ, i % NZ, NX + xx] = p[BR:]
            return carry

        lax.fori_loop(0, NG, step, 0)

    def add(dst, srcs, n=8):
        def step(i, carry):
            v = dst[i].astype(F32)
            for r in srcs:
                v = v + r[i].astype(F32)
            dst[i] = v.astype(BF16)
            return carry

        lax.fori_loop(0, n, step, 0)

    def finish(refs):
        tot = refs[0][...].astype(F32)
        for r in refs[1:]:
            tot = tot + r[...].astype(F32)
        out_ref[...] = (mine[...].astype(F32) + tot).astype(BF16)

    xs = (xo, xr, xl, x)
    zs = [(z + half) % NZ]
    for k in range(half - 1, 0, -1):
        zs += [(z + k) % NZ, (z + NZ - k) % NZ]
    zs.append(z)
    ys = ((y + 2) % NY, (y + 1) % NY, (y + NY - 1) % NY, y)
    yright, yleft = y_dev((y + 1) % NY), y_dev((y + NY - 1) % NY)

    def quad(ref, i, j):
        return ref.at[ys[j] // 2, zs[i], pl.ds((ys[j] % 2) * NX, NX)]

    @pl.when(s == 0)
    def _():
        mark = len(sent)

        def give(i):
            for h in range(2):
                down_plane(tsend, 1, zs[i], h)
            for j in range(4):
                n = 4 * i + j
                start(_remote(quad(tsend, i, j), quad(pbuf, i, j), cpsend.at[n], cprecv.at[n], partner))

        def at(ref, i, j):
            yy = ys[j]
            return ref.at[yy // 2, :, (yy % 2) * NX + xs[i]]

        def take(i, j, more=()):
            landed(at(pbuf, i, j), cprecv.at[4 * i + j])
            add(at(acc, i, j), [at(pbuf, i, j)] + list(more))

        right, left = x_dev(xr), x_dev(xl)
        give(0)
        down_group(acc, 0, xs[0])
        give(1)
        for j in range(4):
            take(0, j)
            start(_remote(at(acc, 0, j), ring.at[j], crsend.at[j], crrecv.at[j], right if j % 2 == 0 else left))
        down_group(acc, 0, xs[1])
        give(2)
        down_group(acc, 0, xs[2])
        give(3)
        for j in range(4):
            for i, way, dev in ((1, 0, right), (2, 1, left)):
                if j % 2 == way:
                    landed(ring.at[j], crrecv.at[j])
                    take(i, j, [ring.at[j]])
                else:
                    take(i, j)
                k = 4 + 4 * way + j
                start(_remote(at(acc, i, j), ring.at[k], crsend.at[k], crrecv.at[k], dev))
            give(4 + j)
        down_group(acc, 0, xs[3])
        for j in range(4):
            landed(ring.at[4 + j], crrecv.at[4 + j])
            landed(ring.at[8 + j], crrecv.at[8 + j])
            take(3, j, [ring.at[4 + j], ring.at[8 + j]])
            yy = ys[j]
            tt = (yy % 2) * NX + x
            if j == 0:
                for w in range(2):
                    part4 = pl.ds(4 * w, 4)
                    start(
                        _remote(
                            acc.at[yy // 2, part4, tt],
                            ybuf.at[0, part4],
                            cysend.at[w],
                            cyrecv.at[w],
                            (yright, yleft)[w],
                        )
                    )
            elif j < 3:
                w = j - 1
                part4 = pl.ds(4 * w, 4)
                landed(ybuf.at[0, part4], cyrecv.at[w])
                add(acc.at[yy // 2, part4, tt], [ybuf.at[0, part4]], 4)
                start(
                    _remote(at(acc, 3, j), ybuf.at[j], cysend.at[1 + j], cyrecv.at[1 + j], (yright, yleft)[w])
                )
        for j in (1, 2):
            landed(ybuf.at[j], cyrecv.at[1 + j])
        add(at(acc, 3, 3), [ybuf.at[1], ybuf.at[2]])
        for o in range(1, NZ):
            e = (z + o) % NZ
            start(_remote(acc.at[yh, e, t], fbuf.at[o], cfsend.at[o], cfrecv.at[o], z_dev(e)))
        for o in range(1, NZ):
            landed(fbuf.at[o], cfrecv.at[o])
        finish([acc.at[yh, z, t]] + [fbuf.at[o] for o in range(1, NZ)])
        for c in sent[mark:]:
            c.wait_send()
        del sent[mark:]

    @pl.when(s == 1)
    def _():
        mark = len(sent)

        def give(i):
            down_group(tsend, 0, xs[i])
            for j, yy in enumerate(ys):
                tt = (yy % 2) * NX + xs[i]
                n = 4 * i + j
                start(
                    _remote(tsend.at[yy // 2, :, tt], pbuf.at[yy // 2, :, tt], cpsend.at[n], cprecv.at[n], partner)
                )

        def have(i):
            for h in range(2):
                down_plane(acc, 1, zs[i], h)

        def take(i, j, more=()):
            landed(quad(pbuf, i, j), cprecv.at[4 * i + j])
            add(quad(acc, i, j), [quad(pbuf, i, j)] + list(more), NX)

        def slot(n):
            return ring.at[n // 2, pl.ds((n % 2) * NX, NX)]

        right, left = z_dev(zr), z_dev(zl)
        give(0)
        have(0)
        for j in range(4):
            take(0, j)
            start(_remote(quad(acc, 0, j), slot(j), crsend.at[j], crrecv.at[j], (right, left)[j % 2]))
        have(1)
        have(2)
        give(1)
        for k in range(1, half):
            for j in range(4):
                for way, dev in ((0, right), (1, left)):
                    i = 2 * k - 1 + way
                    prev = 4 + 8 * (k - 2) + 4 * way + j
                    if k == 1:
                        prev = j if j % 2 == way else None
                    if prev is None:
                        take(i, j)
                    else:
                        landed(slot(prev), crrecv.at[prev])
                        take(i, j, [slot(prev)])
                    q = 4 + 8 * (k - 1) + 4 * way + j
                    start(_remote(quad(acc, i, j), slot(q), crsend.at[q], crrecv.at[q], dev))
            if k == 1:
                give(2)
                give(3)
            have(2 * k + 1)
            if k < half - 1:
                have(2 * k + 2)

        for j in range(4):
            q = 4 + 8 * (half - 2) + j
            landed(slot(q), crrecv.at[q])
            landed(slot(q + 4), crrecv.at[q + 4])
            take(7, j, [slot(q), slot(q + 4)])
            oy = (2, 1, 3, 0)[j]
            for ox in range(NX):
                if oy + ox:
                    n = oy * NX + ox
                    ex = (x + ox) % NX
                    src = acc.at[ys[j] // 2, z, (ys[j] % 2) * NX + ex]
                    start(_remote(src, fbuf.at[n], cfsend.at[n], cfrecv.at[n], xy_dev(ex, ys[j])))
        for n in range(1, NY * NX):
            landed(fbuf.at[n], cfrecv.at[n])
        finish([acc.at[yh, z, t]] + [fbuf.at[n] for n in range(1, NY * NX)])
        for c in sent[mark:]:
            c.wait_send()
        del sent[mark:]

    for o in range(1, NST):
        e = (d + o) % NST
        _remote(part.at[e], rbuf.at[d], bsend.at[e], brecv.at[d], st_dev(e)).wait_send()
    for c in sent:
        c.wait_send()


def layer(queries, latent_cache, cache_len, value_up, out_proj, residual, w_gate, w_up, w_down, route_ids, route_weights):
    vmem = pl.BlockSpec(memory_space=pltpu.VMEM)
    hbm = pl.BlockSpec(memory_space=pl.ANY)
    dma = pltpu.SemaphoreType.DMA
    depth = value_up.shape[0] * VDIM
    scratch = [
        pltpu.VMEM((BR, latent_cache.shape[2], latent_cache.shape[1]), BF16),
        pltpu.VMEM(value_up.shape, BF16),
        pltpu.VMEM((BR // 2, queries.shape[1], latent_cache.shape[1]), F32),
        pltpu.VMEM((BR // 2, queries.shape[1], LAT), F32),
        pltpu.VMEM((2, BR // 2, depth), BF16),
        pltpu.VMEM((NG, 2, BR // 2, depth), BF16),
        pltpu.VMEM((depth, BC), BF16),
        pltpu.VMEM(w_gate.shape[:1] + (256,), BF16),
        pltpu.VMEM(w_down.shape, BF16),
        pltpu.VMEM((NG, 128, BC), BF16),
        pltpu.VMEM((128, BC), BF16),
        pltpu.VMEM((NST * BR, 8), F32),
        pltpu.VMEM((NST, BR, BC), BF16),
        pltpu.VMEM((NST, BR, BC), BF16),
        pltpu.VMEM((BR, BC), BF16),
        pltpu.VMEM((2, NZ, 2, NT, BR, BC), BF16),
        pltpu.VMEM((2, NT, BR, 256), F32),
        pltpu.VMEM((2, NT, BR, 128), BF16),
        pltpu.VMEM((2, NZ, NT, BR, BC), BF16),
        pltpu.VMEM((2, NZ, NT, BR, BC), BF16),
        pltpu.VMEM((2, NZ, NT, BR, BC), BF16),
        pltpu.VMEM((16, 8, BR, BC), BF16),
        pltpu.VMEM((3, 8, BR, BC), BF16),
        pltpu.VMEM((16, BR, BC), BF16),
        dma((3,)),
        dma((3,)),
        dma((NG, 2, 5)),
        dma((NG, 2)),
        dma((1,)),
        dma((NST,)),
        dma((NST,)),
        dma((16,)),
        dma((16,)),
        dma((NY,)),
        dma((NY,)),
        dma((2, 16)),
        dma((2, 16)),
        dma((32,)),
        dma((32,)),
        dma((32,)),
        dma((32,)),
        dma((28,)),
        dma((28,)),
        dma((4,)),
        dma((4,)),
        dma((16,)),
        dma((16,)),
    ]
    return pl.pallas_call(
        _layer_kernel,
        out_shape=jax.ShapeDtypeStruct((BR, BC), BF16),
        in_specs=[pl.BlockSpec(memory_space=pltpu.SMEM), vmem, hbm, hbm, vmem, vmem, hbm, hbm, hbm, vmem, vmem],
        out_specs=vmem,
        scratch_shapes=scratch,
        compiler_params=pltpu.CompilerParams(
            collective_id=0, has_side_effects=True, vmem_limit_bytes=60 * 1024 * 1024
        ),
        name="layer",
    )(
        cache_len,
        queries,
        latent_cache.transpose(0, 2, 1),
        value_up,
        out_proj.T,
        residual.T,
        w_gate,
        w_up,
        w_down,
        route_ids.T,
        route_weights.T,
    )


def on_device(
    queries,
    latent_cache,
    cache_len,
    value_up,
    out_proj,
    residual,
    w_gate,
    w_up,
    w_down,
    route_ids,
    route_weights,
):
    return layer(
        queries,
        latent_cache,
        cache_len,
        value_up,
        out_proj,
        residual,
        w_gate[0],
        w_up[0],
        w_down[0],
        route_ids,
        route_weights,
    )


def solution(mesh):
    return jax.shard_map(
        on_device,
        mesh=mesh,
        in_specs=(
            P("grp", ("sect", "tp"), None),
            P("grp", None, None),
            P("grp"),
            P(("sect", "tp"), None, None),
            P(("sect", "tp"), "grp"),
            P(None, "grp"),
            P("grp", None, ("sect", "tp")),
            P("grp", None, ("sect", "tp")),
            P("grp", ("sect", "tp"), None),
            P(),
            P(),
        ),
        out_specs=P(("sect", "tp"), "grp"),
        check_vma=False,
    )
```

time: 127 us -> 118 us (0.929)
  the two profiles are of different devices: /device:TPU:1 before, /device:TPU:24 now
where the time goes in v3:
time: 118 us
  Pallas kernels  117 us (99%)
  local copies, waits for them, and re-layouts  1.38 us (1%)
    pallas_call x1, Pallas kernels, layer(): pl.pallas_call(_layer_kernel, out_shape=jax.ShapeDtypeStruct((BR, BC), BF...  117 us

profile of v3, /device:TPU:24, one launch (start us, length us, event | category | flops | bytes accessed | tf_op | source)
XLA Modules:
  0.0 118.0 jit_solution(17763537091327212616)
XLA Ops:
  0.0 116.6 %layer.1 = bf16[32,448]{1,0:T(8,128)(2,1)} custom-call(s32[32]{0:T(128)} %len_ref.1, bf16[32,8,576]{2,1,0:T(8,128)(2,1)} %q_ref.1, bf16[32,576,128]{2,1,0:T(8,128)(2,1)} %bitcast.8, bf16[8,512,128]{2,1,0:T(8,128)(2,1)} %vup_ref.1, bf16[448,1024]{1,0:T(8,128)(2,1)} %bitcast.12, bf16[448,512]{1,0:T(8,128)(2,1)} %bitcast.13, bf16[7168,128]{1,0:T(8,128)(2,1)} %bitcast.9, ...), custom_call_target="tpu_custom_call" | custom-call | tf_op jit(solution)/shard_map/layer/pallas_call | solution.py:726
  116.6 1.4 %copy.13 = bf16[32,448]{1,0:T(8,128)(2,1)} copy(bf16[32,448]{1,0:T(8,128)(2,1)} %layer.1) | data formatting | bytes 57344

commit v4 on v3

--- a/solution.py
+++ b/solution.py
@@ -15,6 +15,9 @@
 NST = 16
 BR = 32
 BC = 448
+TILE = 16
+PACK = 7 * TILE
+WIDE = 512
 
 SOFTMAX_SCALE = 0.0721688
 MASK_VALUE = -1e30
@@ -81,6 +84,7 @@
     ring,
     ybuf,
     fbuf,
+    tmp,
     csem,
     wsem,
     hsend,
@@ -141,9 +145,15 @@
     for c in (fetch[0], fetch[2], fetch[1]):
         c.start()
     loads = [
-        pltpu.make_async_copy(wg_ref, wbuf.at[:, pl.ds(0, 128)], wsem.at[0]),
-        pltpu.make_async_copy(wu_ref, wbuf.at[:, pl.ds(128, 128)], wsem.at[1]),
+        pltpu.make_async_copy(wg_ref, wbuf.at[:, pl.ds(0, BC), pl.ds(0, 128)], wsem.at[0]),
+        pltpu.make_async_copy(wu_ref, wbuf.at[:, pl.ds(0, BC), pl.ds(128, 128)], wsem.at[1]),
         pltpu.make_async_copy(wd_ref, wdraw, wsem.at[2]),
+        pltpu.make_async_copy(
+            wg_ref.at[:, pl.ds(384, 64)], wbuf.at[:, pl.ds(BC, 64), pl.ds(0, 128)], wsem.at[3]
+        ),
+        pltpu.make_async_copy(
+            wu_ref.at[:, pl.ds(384, 64)], wbuf.at[:, pl.ds(BC, 64), pl.ds(128, 128)], wsem.at[4]
+        ),
     ]
     for c in loads:
         c.start()
@@ -262,12 +272,19 @@
             project(held, blocks)
             held, blocks = [], []
 
+    def twice(v, high):
+        v = v.astype(F32)
+        low = lax.broadcasted_iota(jnp.int32, v.shape, 1) < 64
+        return jnp.where(low != high, v, pltpu.roll(v, 64, 1)).astype(BF16)
+
     for c in loads:
         c.wait()
     for i in range(8):
         v = wdraw[:, pl.ds(2 * BC * i, 2 * BC)]
-        wdbuf[2 * i] = v[:, :BC]
-        wdbuf[2 * i + 1] = v[:, BC:]
+        wdbuf[2 * i, :, :384] = v[:, :384]
+        wdbuf[2 * i, :, 384:] = twice(v[:, 384:512], False)
+        wdbuf[2 * i + 1, :, :384] = v[:, BC : BC + 384]
+        wdbuf[2 * i + 1, :, 384:] = twice(v[:, 768:896], True)
 
     base = pl.multiple_of((d % 4) * BR, BR)
     total = resbuf[pl.ds(base, BR), :].astype(F32) + part[d].astype(F32)
@@ -275,12 +292,43 @@
         e = (d + NST - o) % NST
         landed(rbuf.at[e], brecv.at[e])
         total = total + rbuf[e].astype(F32)
-    mine[...] = total.astype(BF16)
-    rows[yh, z, s, t] = total.astype(BF16)
+    left_half = lax.broadcasted_iota(jnp.int32, (TILE, 128), 1) < 64
+    tmp[...] = jnp.zeros_like(tmp)
+    tmp[:, :BC] = total
+    tails = tmp[:, 384:]
+    own_tiles = [tmp[TILE * r : TILE * (r + 1), 128 * c : 128 * (c + 1)] for r in range(2) for c in range(3)]
+    own_tiles.append(jnp.where(left_half, tails[:TILE], pltpu.roll(tails[TILE:], 64, 1)))
+    packed = jnp.concatenate(own_tiles, axis=0).astype(BF16)
+    mine[...] = packed
+    rows[yh, z, s, t] = packed
     hacc[...] = jnp.zeros_like(hacc)
 
     def weights(hh, zz):
-        return wbuf[pl.ds(pl.multiple_of((hh * NZ + zz) * BC, BC), BC), :]
+        return wbuf[hh * NZ + zz]
+
+    def matrix(blocks):
+        lanes = lax.broadcasted_iota(jnp.int32, (TILE, 128), 1) < 64
+
+        def tile(b, i):
+            return b[TILE * i : TILE * (i + 1), :]
+
+        columns = [
+            jnp.concatenate([tile(b, 3 * r + c) for b in blocks for r in range(2)], axis=0) for c in range(3)
+        ]
+        last = []
+        for b in blocks:
+            v = tile(b, 6)
+            last += [jnp.where(lanes, v, jnp.zeros_like(v)), jnp.where(lanes, jnp.zeros_like(v), v)]
+        return jnp.concatenate(columns + [jnp.concatenate(last, axis=0)], axis=1)
+
+    def put(dst, p):
+        for r in range(2):
+            for c in range(3):
+                n = 3 * r + c
+                dst[TILE * n : TILE * (n + 1), :] = p[TILE * r : TILE * (r + 1), 128 * c : 128 * (c + 1)].astype(
+                    BF16
+                )
+        dst[TILE * 6 :, :] = jnp.where(left_half, p[:TILE, 384:], p[TILE:, 384:]).astype(BF16)
 
     def use_plane(k):
         count = 2 if k in (0, half) else 4
@@ -288,7 +336,7 @@
         def step(i, carry):
             hh = i % 2
             zz = (z + (i // 2) * 2 * k + NZ - k) % NZ
-            a = rows[hh, zz, 1].reshape(8 * BR, BC)
+            a = matrix([rows.at[hh, zz, 1, e] for e in range(NT)])
             p = jnp.dot(a, weights(hh, zz), preferred_element_type=F32)
             hacc[1] += p.reshape(8, BR, 256)
             return carry
@@ -301,7 +349,7 @@
         def step(i, carry):
             hh = i // NZ
             zz = i % NZ
-            a = jnp.concatenate([rows[hh, zz, 0, e] for e in places], axis=0)
+            a = matrix([rows.at[hh, zz, 0, e] for e in places])
             return carry + jnp.dot(a, weights(hh, zz), preferred_element_type=F32)
 
         p = lax.fori_loop(0, NG, step, jnp.zeros((len(places) * BR, 256), F32))
@@ -469,15 +517,16 @@
     def down_plane(dst, sec, zz, hh):
         a = hid[sec].reshape(NT * BR, 128)
         p = jnp.dot(a, wdbuf[hh * NZ + zz], preferred_element_type=F32)
-        dst[hh, zz] = p.astype(BF16).reshape(NT, BR, BC)
+        for e in range(NT):
+            put(dst.at[hh, zz, e], p[BR * e : BR * (e + 1)])
 
     def down_group(dst, sec, xx):
         a = jnp.concatenate([hid[sec, xx], hid[sec, NX + xx]], axis=0)
 
         def step(i, carry):
-            p = jnp.dot(a, wdbuf[i], preferred_element_type=F32).astype(BF16)
-            dst[i // NZ, i % NZ, xx] = p[:BR]
-            dst[i // NZ, i % NZ, NX + xx] = p[BR:]
+            p = jnp.dot(a, wdbuf[i], preferred_element_type=F32)
+            put(dst.at[i // NZ, i % NZ, xx], p[:BR])
+            put(dst.at[i // NZ, i % NZ, NX + xx], p[BR:])
             return carry
 
         lax.fori_loop(0, NG, step, 0)
@@ -496,7 +545,14 @@
         tot = refs[0][...].astype(F32)
         for r in refs[1:]:
             tot = tot + r[...].astype(F32)
-        out_ref[...] = (mine[...].astype(F32) + tot).astype(BF16)
+        tot = mine[...].astype(F32) + tot
+        for r in range(2):
+            for c in range(3):
+                n = TILE * (3 * r + c)
+                out_ref[TILE * r : TILE * (r + 1), 128 * c : 128 * (c + 1)] = tot[n : n + TILE].astype(BF16)
+        tails = tot[6 * TILE :]
+        out_ref[:TILE, 384:] = tails[:, :64].astype(BF16)
+        out_ref[TILE:, 384:] = pltpu.roll(tails, 64, 1)[:, :64].astype(BF16)
 
     xs = (xo, xr, xl, x)
     zs = [(z + half) % NZ]
@@ -682,25 +738,26 @@
         pltpu.VMEM((2, BR // 2, depth), BF16),
         pltpu.VMEM((NG, 2, BR // 2, depth), BF16),
         pltpu.VMEM((depth, BC), BF16),
-        pltpu.VMEM(w_gate.shape[:1] + (256,), BF16),
+        pltpu.VMEM((NG, WIDE, 256), BF16),
         pltpu.VMEM(w_down.shape, BF16),
-        pltpu.VMEM((NG, 128, BC), BF16),
+        pltpu.VMEM((NG, 128, WIDE), BF16),
         pltpu.VMEM((128, BC), BF16),
         pltpu.VMEM((NST * BR, 8), F32),
         pltpu.VMEM((NST, BR, BC), BF16),
         pltpu.VMEM((NST, BR, BC), BF16),
-        pltpu.VMEM((BR, BC), BF16),
-        pltpu.VMEM((2, NZ, 2, NT, BR, BC), BF16),
+        pltpu.VMEM((PACK, 128), BF16),
+        pltpu.VMEM((2, NZ, 2, NT, PACK, 128), BF16),
         pltpu.VMEM((2, NT, BR, 256), F32),
         pltpu.VMEM((2, NT, BR, 128), BF16),
-        pltpu.VMEM((2, NZ, NT, BR, BC), BF16),
-        pltpu.VMEM((2, NZ, NT, BR, BC), BF16),
-        pltpu.VMEM((2, NZ, NT, BR, BC), BF16),
-        pltpu.VMEM((16, 8, BR, BC), BF16),
-        pltpu.VMEM((3, 8, BR, BC), BF16),
-        pltpu.VMEM((16, BR, BC), BF16),
+        pltpu.VMEM((2, NZ, NT, PACK, 128), BF16),
+        pltpu.VMEM((2, NZ, NT, PACK, 128), BF16),
+        pltpu.VMEM((2, NZ, NT, PACK, 128), BF16),
+        pltpu.VMEM((16, 8, PACK, 128), BF16),
+        pltpu.VMEM((3, 8, PACK, 128), BF16),
+        pltpu.VMEM((16, PACK, 128), BF16),
+        pltpu.VMEM((BR, WIDE), F32),
         dma((3,)),
-        dma((3,)),
+        dma((5,)),
         dma((NG, 2, 5)),
         dma((NG, 2)),
         dma((1,)),
@@ -740,8 +797,8 @@
         value_up,
         out_proj.T,
         residual.T,
-        w_gate,
-        w_up,
+        w_gate.reshape(NG, BC, 128),
+        w_up.reshape(NG, BC, 128),
         w_down,
         route_ids.T,
         route_weights.T,

time: 118 us -> 113 us (0.958)
  Pallas kernels: 117 us -> 111 us
    pallas_call x1, Pallas kernels: 117 us -> 111 us  [layer(): pl.pallas_call(_layer_kernel, out_shape=jax.ShapeDtypeStruct((BR, BC), BF...]
where the time goes in v4:
time: 113 us
  Pallas kernels  111 us (98%)
  local copies, waits for them, and re-layouts  1.38 us (1%)
    pallas_call x1, Pallas kernels, layer(): pl.pallas_call(_layer_kernel, out_shape=jax.ShapeDtypeStruct((BR, BC), BF...  111 us

profile of v4, /device:TPU:24, one launch (start us, length us, event | category | flops | bytes accessed | tf_op | source)
XLA Modules:
  0.0 112.7 jit_solution(3559759185162903765)
XLA Ops:
  0.0 111.3 %layer.1 = bf16[32,448]{1,0:T(8,128)(2,1)} custom-call(s32[32]{0:T(128)} %len_ref.1, bf16[32,8,576]{2,1,0:T(8,128)(2,1)} %q_ref.1, bf16[32,576,128]{2,1,0:T(8,128)(2,1)} %bitcast.8, bf16[8,512,128]{2,1,0:T(8,128)(2,1)} %vup_ref.1, bf16[448,1024]{1,0:T(8,128)(2,1)} %bitcast.12, bf16[448,512]{1,0:T(8,128)(2,1)} %bitcast.13, bf16[16,448,128]{2,1,0:T(8,128)(2,1)} %bitcast.9, ...), custom_call_target="tpu_custom_call" | custom-call | tf_op jit(solution)/shard_map/layer/pallas_call | solution.py:783
  111.3 1.4 %copy.13 = bf16[32,448]{1,0:T(8,128)(2,1)} copy(bf16[32,448]{1,0:T(8,128)(2,1)} %layer.1) | data formatting | bytes 57344

commit v5 on v4

--- a/solution.py
+++ b/solution.py
@@ -520,13 +520,14 @@
         for e in range(NT):
             put(dst.at[hh, zz, e], p[BR * e : BR * (e + 1)])
 
-    def down_group(dst, sec, xx):
-        a = jnp.concatenate([hid[sec, xx], hid[sec, NX + xx]], axis=0)
+    def down_group(dst, sec, *xx):
+        places = [o + e for e in xx for o in (0, NX)]
+        a = jnp.concatenate([hid[sec, e] for e in places], axis=0)
 
         def step(i, carry):
             p = jnp.dot(a, wdbuf[i], preferred_element_type=F32)
-            put(dst.at[i // NZ, i % NZ, xx], p[:BR])
-            put(dst.at[i // NZ, i % NZ, NX + xx], p[BR:])
+            for n, e in enumerate(places):
+                put(dst.at[i // NZ, i % NZ, e], p[n * BR : (n + 1) * BR])
             return carry
 
         lax.fori_loop(0, NG, step, 0)
@@ -649,14 +650,17 @@
     def _():
         mark = len(sent)
 
-        def give(i):
-            down_group(tsend, 0, xs[i])
+        def give(*ii):
+            down_group(tsend, 0, *[xs[i] for i in ii])
             for j, yy in enumerate(ys):
-                tt = (yy % 2) * NX + xs[i]
-                n = 4 * i + j
-                start(
-                    _remote(tsend.at[yy // 2, :, tt], pbuf.at[yy // 2, :, tt], cpsend.at[n], cprecv.at[n], partner)
-                )
+                for i in ii:
+                    tt = (yy % 2) * NX + xs[i]
+                    n = 4 * i + j
+                    start(
+                        _remote(
+                            tsend.at[yy // 2, :, tt], pbuf.at[yy // 2, :, tt], cpsend.at[n], cprecv.at[n], partner
+                        )
+                    )
 
         def have(i):
             for h in range(2):
@@ -677,7 +681,7 @@
             start(_remote(quad(acc, 0, j), slot(j), crsend.at[j], crrecv.at[j], (right, left)[j % 2]))
         have(1)
         have(2)
-        give(1)
+        give(1, 2)
         for k in range(1, half):
             for j in range(4):
                 for way, dev in ((0, right), (1, left)):
@@ -693,7 +697,6 @@
                     q = 4 + 8 * (k - 1) + 4 * way + j
                     start(_remote(quad(acc, i, j), slot(q), crsend.at[q], crrecv.at[q], dev))
             if k == 1:
-                give(2)
                 give(3)
             have(2 * k + 1)
             if k < half - 1:

time: 113 us -> 110 us (0.973)
  Pallas kernels: 111 us -> 109 us
    pallas_call x1, Pallas kernels: 111 us -> 109 us  [layer(): pl.pallas_call(_layer_kernel, out_shape=jax.ShapeDtypeStruct((BR, BC), BF...]
where the time goes in v5:
time: 110 us
  Pallas kernels  109 us (99%)
  local copies, waits for them, and re-layouts  1.38 us (1%)
    pallas_call x1, Pallas kernels, layer(): pl.pallas_call(_layer_kernel, out_shape=jax.ShapeDtypeStruct((BR, BC), BF...  109 us

profile of v5, /device:TPU:24, one launch (start us, length us, event | category | flops | bytes accessed | tf_op | source)
XLA Modules:
  0.0 109.9 jit_solution(16946648989541635544)
XLA Ops:
  0.0 108.5 %layer.1 = bf16[32,448]{1,0:T(8,128)(2,1)} custom-call(s32[32]{0:T(128)} %len_ref.1, bf16[32,8,576]{2,1,0:T(8,128)(2,1)} %q_ref.1, bf16[32,576,128]{2,1,0:T(8,128)(2,1)} %bitcast.8, bf16[8,512,128]{2,1,0:T(8,128)(2,1)} %vup_ref.1, bf16[448,1024]{1,0:T(8,128)(2,1)} %bitcast.12, bf16[448,512]{1,0:T(8,128)(2,1)} %bitcast.13, bf16[16,448,128]{2,1,0:T(8,128)(2,1)} %bitcast.9, ...), custom_call_target="tpu_custom_call" | custom-call | tf_op jit(solution)/shard_map/layer/pallas_call | solution.py:786
  108.6 1.4 %copy.13 = bf16[32,448]{1,0:T(8,128)(2,1)} copy(bf16[32,448]{1,0:T(8,128)(2,1)} %layer.1) | data formatting | bytes 57344
